TPU v7x, 512 devices: a whole 4x8x8 slice. The times are simulated.
512 devices in a mesh: sky: 64 (over x, z, core), exp: 8 (over y).
Axes of the slice: x: 4, y: 8, z: 8, core: 2. Of those that a mesh axis runs over, the one named last changes fastest.
Arguments:
- padded_tiles: bfloat16 [24576, 10752], P(('sky', 'exp')), may hold values from -6 to 6
- coefficients: float32 [24576, 20], P(('sky', 'exp')), may hold values from -1.8 to 1.8
- row_taps: bfloat16 [24576, 6, 24], P(('sky', 'exp')), may hold values from 0.019897461 to 0.34960938
- col_taps: bfloat16 [24576, 6, 128], P(('sky', 'exp')), may hold values from 0.019897461 to 0.34960938
- shifts: int32 [24576, 2], P(('sky', 'exp')), may hold values from 0 to 2
- mask_words: int32 [24576], P(('sky', 'exp')), may hold values from -2147483648 to 2147483646
- weights: bfloat16 [24576], P(('sky', 'exp')), may hold values from 0.049804688 to 0.5
- destination: int32 [24576, 1], P(('sky', 'exp')), may hold values from 0 to 63; in each aligned block of 48 rows (0 to 47, 48 to 95, ...) at most 2 rows name the same one
- patch_slot: int32 [24576], P(('sky', 'exp')), may hold values from 0 to 15
- basis_rows: bfloat16 [20, 41], replicated, may hold values from -1 to 1
- basis_cols: bfloat16 [20, 41], replicated, may hold values from -1 to 1
Outputs:
- coadd: float32 [24576, 128], P(('sky', 'exp'))
Inputs may be any that keep to these rules, and one draw needn't show every extreme that they name: `destination`: the 48 tiles of one device name one patch at most 2 times, a bound that some block reaches.
All inputs are finite; a program needn't handle non-finite values.
Results may differ from a plain program's by a relative error of at most 0.014.
Values may be sent and summed in bfloat16 or wider, within the bound.
No kernel may reach another device: no remote copies, remote signals or barrier semaphores. Data moves between devices by JAX's collectives and lax.ppermute only.
A program may use at most 64 MiB of HBM per device.

v0:
```python
import jax
import jax.numpy as jnp
from jax import lax
from jax.sharding import PartitionSpec as P

SLOTS = 16


def toeplitz(basis_vals, distance):
    kernel_len = basis_vals.shape[1]
    picks = (distance[:, :, None] == jnp.arange(kernel_len, dtype=jnp.int32)[None, None, :]).astype(
        jnp.float32
    )
    return jnp.einsum("xyk,bk->bxy", picks, basis_vals.astype(jnp.float32)).astype(jnp.bfloat16)


def build_tables(basis_rows, basis_cols, tile_rows, tile_cols):
    kernel_len = basis_rows.shape[1]
    out_rows = jnp.arange(tile_rows, dtype=jnp.int32)
    in_rows = jnp.arange(tile_rows + kernel_len - 1, dtype=jnp.int32)
    out_cols = jnp.arange(tile_cols, dtype=jnp.int32)
    in_cols = jnp.arange(tile_cols + kernel_len - 1, dtype=jnp.int32)
    row_toeplitz = toeplitz(basis_rows, in_rows[None, :] - out_rows[:, None])
    col_toeplitz = toeplitz(basis_cols, in_cols[:, None] - out_cols[None, :])
    return (row_toeplitz, col_toeplitz)


def band_matrix(tap_values, band_shift):
    tap_count = tap_values.shape[1]
    length = tap_values.shape[2]
    positions = jnp.arange(length, dtype=jnp.int32)
    band_start = jnp.clip(
        positions[None, :] + band_shift[:, None] - tap_count // 2, 0, length - tap_count
    )
    band_offset = positions[None, None, :] - band_start[:, :, None]
    matrix = jnp.zeros((tap_values.shape[0], length, length), tap_values.dtype)
    for tap_index in range(tap_count):
        matrix = matrix + jnp.where(
            band_offset == tap_index,
            tap_values[:, tap_index, :][:, :, None],
            jnp.zeros((), tap_values.dtype),
        )
    return matrix


def mask_good(mask_words, tile_rows, tile_cols):
    bit_index = jnp.arange(32, dtype=jnp.int32)
    flagged = jnp.bitwise_and(jnp.right_shift(mask_words[:, None], bit_index[None, :]), 1)
    good_cells = (1 - flagged).astype(jnp.float32).reshape(mask_words.shape[0], 4, 8)
    good_cells = jnp.repeat(good_cells, tile_rows // 4, axis=1)
    return jnp.repeat(good_cells, tile_cols // 8, axis=2)


def body(
    padded_tiles,
    coefficients,
    row_taps,
    col_taps,
    shifts,
    mask_words,
    weights,
    destination,
    patch_slot,
    basis_rows,
    basis_cols,
):
    sky_count = lax.axis_size("sky")
    tiles_dev = padded_tiles.shape[0]
    tile_rows = row_taps.shape[2]
    tile_cols = col_taps.shape[2]
    kernel_len = basis_rows.shape[1]
    slot_count = SLOTS
    capacity = 2 * ((tiles_dev + sky_count - 1) // sky_count)
    row_toeplitz, col_toeplitz = build_tables(basis_rows, basis_cols, tile_rows, tile_cols)
    per_block = 8
    block_count = tiles_dev // per_block

    def match_and_warp(tile_group):
        padded, coef_block, rtap, ctap, shift_block = tile_group
        padded = padded.reshape(per_block, tile_rows + kernel_len - 1, tile_cols + kernel_len - 1)
        row_pass = jnp.einsum(
            "bic,ncj->nbij", row_toeplitz, padded, preferred_element_type=jnp.float32
        )
        scaled = (row_pass * coef_block[:, :, None, None]).astype(jnp.bfloat16)
        matched = jnp.einsum(
            "nbij,bjk->nik", scaled, col_toeplitz, preferred_element_type=jnp.float32
        ).astype(jnp.bfloat16)
        row_warp = band_matrix(rtap, shift_block[:, 0])
        col_warp = band_matrix(ctap, shift_block[:, 1])
        halfway = jnp.einsum(
            "nij,njk->nik", row_warp, matched, preferred_element_type=jnp.float32
        ).astype(jnp.bfloat16)
        return jnp.einsum(
            "nij,nkj->nik", halfway, col_warp, preferred_element_type=jnp.float32
        ).astype(jnp.bfloat16)

    inputs = (padded_tiles, coefficients, row_taps, col_taps, shifts)
    grouped = tuple((arr.reshape((block_count, per_block) + arr.shape[1:]) for arr in inputs))
    warped = lax.map(match_and_warp, grouped).reshape(tiles_dev, tile_rows * tile_cols)
    dest_flat = destination[:, 0]
    dest_onehot = (dest_flat[:, None] == jnp.arange(sky_count, dtype=jnp.int32)[None, :]).astype(
        jnp.int32
    )
    before = jnp.cumsum(dest_onehot, axis=0) - dest_onehot
    dest_rank = jnp.sum(before * dest_onehot, axis=1)
    target = dest_flat * capacity + dest_rank
    chosen = jnp.arange(sky_count * capacity, dtype=jnp.int32)[:, None] == target[None, :]
    select = chosen.astype(jnp.bfloat16)
    slot_onehot = (patch_slot[:, None] == jnp.arange(slot_count, dtype=jnp.int32)[None, :]).astype(
        jnp.bfloat16
    )
    send_tiles = jnp.dot(select, warped, preferred_element_type=jnp.float32).astype(jnp.bfloat16)
    good_cells = mask_good(mask_words, tile_rows, tile_cols)
    weight_plane = (
        (weights.astype(jnp.float32)[:, None, None] * good_cells)
        .astype(jnp.bfloat16)
        .reshape(tiles_dev, tile_rows * tile_cols)
    )
    send_planes = jnp.dot(select, weight_plane, preferred_element_type=jnp.float32).astype(
        jnp.bfloat16
    )
    send_slots = jnp.dot(select, slot_onehot, preferred_element_type=jnp.float32).astype(
        jnp.bfloat16
    )
    recv_tiles, recv_planes, recv_slots = (
        lax.all_to_all(send_tiles, "sky", split_axis=0, concat_axis=0, tiled=True),
        lax.all_to_all(send_planes, "sky", split_axis=0, concat_axis=0, tiled=True),
        lax.all_to_all(send_slots, "sky", split_axis=0, concat_axis=0, tiled=True),
    )
    plane_vals = recv_planes.astype(jnp.float32)
    products = plane_vals * recv_tiles.astype(jnp.float32)
    slot_vals = recv_slots.astype(jnp.float32).T
    numerator = jnp.dot(slot_vals, products, precision=lax.Precision.HIGHEST)
    weight_sum = jnp.dot(slot_vals, plane_vals, precision=lax.Precision.HIGHEST)
    numerator = numerator.reshape(slot_count * tile_rows, tile_cols)
    weight_sum = weight_sum.reshape(slot_count * tile_rows, tile_cols)
    totals = (
        lax.psum_scatter(
            numerator.astype(jnp.bfloat16), "exp", scatter_dimension=0, tiled=True
        ).astype(jnp.float32),
        lax.psum_scatter(
            weight_sum.astype(jnp.bfloat16), "exp", scatter_dimension=0, tiled=True
        ).astype(jnp.float32),
    )
    return totals[0] / jnp.maximum(totals[1], 1.0)


def solution(mesh):
    placed = (
        P(("sky", "exp"), None),
        P(("sky", "exp"), None),
        P(("sky", "exp"), None, None),
        P(("sky", "exp"), None, None),
        P(("sky", "exp"), None),
        P(("sky", "exp")),
        P(("sky", "exp")),
        P(("sky", "exp"), None),
        P(("sky", "exp")),
        P(),
        P(),
    )
    return jax.shard_map(
        body, mesh=mesh, in_specs=placed, out_specs=P(("sky", "exp"), None), check_vma=False
    )
```

profile of v0, /device:TPU:2, one launch (start us, length us, event | category | flops | bytes accessed | tf_op | source)
XLA Modules:
  0.0 193.0 jit_solution(2187660516217481814)
XLA Ops:
  8.9 0.9 convolution_convert_fusion.5
  10.5 13.9 %all-to-all-start = ((bf16[64,2,16]{2,1,0:T(2,128)(2,1)}), bf16[64,2,16]{2,1,0:T(2,128)(2,1)S(1)}, u32[]{:S(2)}, u32[]{:S(2)}) async-start(bf16[64,2,16]{2,1,0:T(2,128)(2,1)} %bitcast.26), calls=%async_computation | async-start | bytes 65536 | tf_op jit(solution)/shard_map/all_to_all | solution.py:128
  26.3 1.0 fusion.132
  27.5 1.2 all_to_all.20
  29.7 3.2 %all-to-all-done = bf16[64,2,16]{2,1,0:T(2,128)(2,1)S(1)} async-done(((bf16[64,2,16]{2,1,0:T(2,128)(2,1)}), bf16[64,2,16]{2,1,0:T(2,128)(2,1)S(1)}, u32[]{:S(2)}, u32[]{:S(2)}) %all-to-all-start) | async-done | bytes 4128 | tf_op jit(solution)/shard_map/all_to_all | solution.py:128
  32.9 7.1 %all-to-all-start.1 = ((bf16[64,2,3072]{2,1,0:T(2,128)(2,1)}), bf16[64,2,3072]{2,1,0:T(2,128)(2,1)S(1)}, u32[]{:S(2)}, u32[]{:S(2)}) async-start(bf16[64,2,3072]{2,1,0:T(2,128)(2,1)} %all_to_all.20), calls=%async_computation.1 | async-start | bytes 1572864 | tf_op jit(solution)/shard_map/all_to_all | solution.py:127
  40.0 30.8 %while.13 = (s32[]{:T(128)}, bf16[6,8,24,128]{3,2,1,0:T(8,128)(2,1)S(1)}, s32[6,8,2]{1,0,2:T(8,128)S(1)}, bf16[6,8,6,24]{3,1,0,2:T(8,128)(2,1)S(1)}, bf16[6,8,10...) while((s32[]{:T(128)}, ...), condition=%wide.region_3.4_spmd, body=%wide.region_2.3_spmd.sunk | while | flops 259956800 | bytes 2027581 | solution.py:99
  40.1 0.9 constant_dynamic-slice_fusion.4
  41.8 1.1 fusion.167
  43.8 1.4 fusion.168
  45.2 0.9 constant_dynamic-slice_fusion.4
  46.9 1.1 fusion.167
  48.9 1.4 fusion.168
  50.3 0.9 constant_dynamic-slice_fusion.4
  52.0 1.1 fusion.167
  54.1 1.4 fusion.168
  55.4 0.9 constant_dynamic-slice_fusion.4
  57.2 1.1 fusion.167
  59.2 1.4 fusion.168
  60.6 0.9 constant_dynamic-slice_fusion.4
  62.3 1.1 fusion.167
  64.3 1.4 fusion.168
  65.7 0.9 constant_dynamic-slice_fusion.4
  67.4 1.1 fusion.167
  69.4 1.4 fusion.168
  71.2 1.2 all_to_all.22
  72.4 10.3 %all-to-all-start.2 = ((bf16[64,2,3072]{2,1,0:T(2,128)(2,1)}), bf16[64,2,3072]{2,1,0:T(2,128)(2,1)S(1)}, u32[]{:S(2)}, u32[]{:S(2)}) async-start(bf16[64,2,3072]{2,1,0:T(2,128)(2,1)} %all_to_all.22), calls=%async_computation.2 | async-start | bytes 1572864 | tf_op jit(solution)/shard_map/all_to_all | solution.py:126
  82.9 21.7 %all-to-all-done.2 = bf16[64,2,3072]{2,1,0:T(2,128)(2,1)S(1)} async-done(((bf16[64,2,3072]{2,1,0:T(2,128)(2,1)}), bf16[64,2,3072]{2,1,0:T(2,128)(2,1)S(1)}, u32[]{:S(2)}, u32[]{:S(2)}) %all-to-all-start.2) | async-done | bytes 786464 | tf_op jit(solution)/shard_map/all_to_all | solution.py:126
  104.6 0.9 fusion.124
  107.2 36.5 %reduce-scatter.3.cloned.1.call-done = bf16[48,128]{1,0:T(8,128)(2,1)} async-done(((bf16[384,128]{1,0:T(8,128)(2,1)}), bf16[48,128]{1,0:T(8,128)(2,1)}) %reduce-scatter.3.cloned.1.call-update) | async-done | bytes 12304 | tf_op jit(solution)/shard_map/reduce_scatter | solution.py:138
  143.7 41.1 %reduce-scatter.5.cloned.1.call-done = bf16[48,128]{1,0:T(8,128)(2,1)} async-done(((bf16[384,128]{1,0:T(8,128)(2,1)}), bf16[48,128]{1,0:T(8,128)(2,1)}) %reduce-scatter.5.cloned.1.call-update) | async-done | bytes 12304 | tf_op jit(solution)/shard_map/reduce_scatter | solution.py:141
  184.8 1.3 maximum_divide_fusion
  (100 shorter events, 18.3 us)
Async XLA Ops:
  6.5 19.7 %copy-start = (bf16[20,41]{1,0:T(8,128)(2,1)S(1)}, bf16[20,41]{1,0:T(8,128)(2,1)}, u32[]{:S(2)}) copy-start(bf16[20,41]{1,0:T(8,128)(2,1)} %param.23) | copy-start | bytes 4924
  10.5 22.5 %all-to-all-start = ((bf16[64,2,16]{2,1,0:T(2,128)(2,1)}), bf16[64,2,16]{2,1,0:T(2,128)(2,1)S(1)}, u32[]{:S(2)}, u32[]{:S(2)}) async-start(bf16[64,2,16]{2,1,0:T(2,128)(2,1)} %bitcast.26), calls=%async_computation | async-start | bytes 65536 | tf_op jit(solution)/shard_map/all_to_all | solution.py:128
  25.9 1.4 copy-start.4
  28.6 0.8 copy-start.1
  28.6 0.9 copy-start.2
  28.7 1.0 copy-start.3
  32.9 39.5 %all-to-all-start.1 = ((bf16[64,2,3072]{2,1,0:T(2,128)(2,1)}), bf16[64,2,3072]{2,1,0:T(2,128)(2,1)S(1)}, u32[]{:S(2)}, u32[]{:S(2)}) async-start(bf16[64,2,3072]{2,1,0:T(2,128)(2,1)} %all_to_all.20), calls=%async_computation.1 | async-start | bytes 1572864 | tf_op jit(solution)/shard_map/all_to_all | solution.py:127
  72.4 32.2 %all-to-all-start.2 = ((bf16[64,2,3072]{2,1,0:T(2,128)(2,1)}), bf16[64,2,3072]{2,1,0:T(2,128)(2,1)S(1)}, u32[]{:S(2)}, u32[]{:S(2)}) async-start(bf16[64,2,3072]{2,1,0:T(2,128)(2,1)} %all_to_all.22), calls=%async_computation.2 | async-start | bytes 1572864 | tf_op jit(solution)/shard_map/all_to_all | solution.py:126
  82.7 61.0 %reduce-scatter.3.cloned.1.call-start = ((), (), s32[]{:S(2)}) async-start(), calls=%async_computation.5 | async-start | bytes 110592 | tf_op jit(solution)/shard_map/reduce_scatter | solution.py:138
  106.2 78.6 %reduce-scatter.5.cloned.1.call-start = ((), (), s32[]{:S(2)}) async-start(), calls=%async_computation.6 | async-start | bytes 110592 | tf_op jit(solution)/shard_map/reduce_scatter | solution.py:141
Sparse Core Ops, SparseCore 0:
  106.3 37.3 reduce-scatter.2
  146.5 38.2 reduce-scatter.4
where the time goes:
time: 194 us; the launch traced here: 193 us
  waiting for transfers between devices  103 us (53%)
  starting transfers between devices  31.4 us (16%)
  local copies, waits for them, and re-layouts  20.3 us (10%)
  matrix products  18.8 us (10%)
  between operations  13.5 us (7%)
  other arithmetic  6.02 us (3%)
    reduce_scatter x1, waiting for transfers between devices, body(): lax.psum_scatter(weight_sum.astype(jnp.bfloat16), 'exp', scatter_dimensio...  41.1 us
    reduce_scatter x1, waiting for transfers between devices, body(): lax.psum_scatter(numerator.astype(jnp.bfloat16), 'exp', scatter_dimension...  36.5 us
    all_to_all x1, waiting for transfers between devices, body(): lax.all_to_all(send_tiles, 'sky', split_axis=0, concat_axis=0, tiled=True)  21.7 us
    all_to_all x1, starting transfers between devices, body(): lax.all_to_all(send_slots, 'sky', split_axis=0, concat_axis=0, tiled=True)  13.9 us
    all_to_all x1, starting transfers between devices, body(): lax.all_to_all(send_tiles, 'sky', split_axis=0, concat_axis=0, tiled=True)  10.3 us
    dot_general x6, matrix products, match_and_warp(): jnp.einsum('nij,nkj->nik', halfway, col_warp, preferred_element_type=jnp....  8.12 us
    all_to_all x1, starting transfers between devices, body(): lax.all_to_all(send_planes, 'sky', split_axis=0, concat_axis=0, tiled=True)  7.1 us
    dot_general x6, matrix products, match_and_warp(): jnp.einsum('nbij,bjk->nik', scaled, col_toeplitz, preferred_element_type=...  6.75 us
  transfers between devices with their start and end apart: 5, of which 4 were waited for; matrix products, arithmetic and copies ran while one was open for 18% of the time, Pallas kernels for 0%

commit v1 on v0

--- a/solution.py
+++ b/solution.py
@@ -43,12 +43,10 @@
     return matrix
 
 
-def mask_good(mask_words, tile_rows, tile_cols):
-    bit_index = jnp.arange(32, dtype=jnp.int32)
-    flagged = jnp.bitwise_and(jnp.right_shift(mask_words[:, None], bit_index[None, :]), 1)
-    good_cells = (1 - flagged).astype(jnp.float32).reshape(mask_words.shape[0], 4, 8)
-    good_cells = jnp.repeat(good_cells, tile_rows // 4, axis=1)
-    return jnp.repeat(good_cells, tile_cols // 8, axis=2)
+def spread_cells(cells, tile_rows, tile_cols):
+    grid = cells.reshape(cells.shape[0], 4, 8)
+    grid = jnp.repeat(grid, tile_rows // 4, axis=1)
+    return jnp.repeat(grid, tile_cols // 8, axis=2)
 
 
 def body(
@@ -106,43 +104,39 @@
     target = dest_flat * capacity + dest_rank
     chosen = jnp.arange(sky_count * capacity, dtype=jnp.int32)[:, None] == target[None, :]
     select = chosen.astype(jnp.bfloat16)
-    slot_onehot = (patch_slot[:, None] == jnp.arange(slot_count, dtype=jnp.int32)[None, :]).astype(
+    plane_size = tile_rows * tile_cols
+    bit_index = jnp.arange(32, dtype=jnp.int32)
+    flagged = jnp.bitwise_and(jnp.right_shift(mask_words[:, None], bit_index[None, :]), 1)
+    cell_weights = weights.astype(jnp.float32)[:, None] * (1 - flagged).astype(jnp.float32)
+    products = warped.astype(jnp.float32).reshape(tiles_dev, tile_rows, tile_cols) * spread_cells(
+        cell_weights, tile_rows, tile_cols
+    )
+    payload = jnp.concatenate(
+        [
+            products.reshape(tiles_dev, plane_size).astype(jnp.bfloat16),
+            cell_weights.astype(jnp.bfloat16),
+            patch_slot[:, None].astype(jnp.bfloat16),
+            jnp.zeros((tiles_dev, 128 - 33), jnp.bfloat16),
+        ],
+        axis=1,
+    )
+    send = jnp.dot(select, payload, preferred_element_type=jnp.float32).astype(jnp.bfloat16)
+    send = send.reshape(sky_count, capacity, plane_size + 128)
+    recv = lax.all_to_all(send, "sky", split_axis=0, concat_axis=0, tiled=True)
+    recv = recv.reshape(sky_count * capacity, plane_size + 128)
+    slot_of = recv[:, plane_size + 32].astype(jnp.int32)
+    slot_onehot = (jnp.arange(slot_count, dtype=jnp.int32)[:, None] == slot_of[None, :]).astype(
         jnp.bfloat16
     )
-    send_tiles = jnp.dot(select, warped, preferred_element_type=jnp.float32).astype(jnp.bfloat16)
-    good_cells = mask_good(mask_words, tile_rows, tile_cols)
-    weight_plane = (
-        (weights.astype(jnp.float32)[:, None, None] * good_cells)
-        .astype(jnp.bfloat16)
-        .reshape(tiles_dev, tile_rows * tile_cols)
-    )
-    send_planes = jnp.dot(select, weight_plane, preferred_element_type=jnp.float32).astype(
-        jnp.bfloat16
-    )
-    send_slots = jnp.dot(select, slot_onehot, preferred_element_type=jnp.float32).astype(
-        jnp.bfloat16
-    )
-    recv_tiles, recv_planes, recv_slots = (
-        lax.all_to_all(send_tiles, "sky", split_axis=0, concat_axis=0, tiled=True),
-        lax.all_to_all(send_planes, "sky", split_axis=0, concat_axis=0, tiled=True),
-        lax.all_to_all(send_slots, "sky", split_axis=0, concat_axis=0, tiled=True),
-    )
-    plane_vals = recv_planes.astype(jnp.float32)
-    products = plane_vals * recv_tiles.astype(jnp.float32)
-    slot_vals = recv_slots.astype(jnp.float32).T
-    numerator = jnp.dot(slot_vals, products, precision=lax.Precision.HIGHEST)
-    weight_sum = jnp.dot(slot_vals, plane_vals, precision=lax.Precision.HIGHEST)
-    numerator = numerator.reshape(slot_count * tile_rows, tile_cols)
-    weight_sum = weight_sum.reshape(slot_count * tile_rows, tile_cols)
-    totals = (
-        lax.psum_scatter(
-            numerator.astype(jnp.bfloat16), "exp", scatter_dimension=0, tiled=True
-        ).astype(jnp.float32),
-        lax.psum_scatter(
-            weight_sum.astype(jnp.bfloat16), "exp", scatter_dimension=0, tiled=True
-        ).astype(jnp.float32),
-    )
-    return totals[0] / jnp.maximum(totals[1], 1.0)
+    sums = jnp.dot(slot_onehot, recv, preferred_element_type=jnp.float32).astype(jnp.bfloat16)
+    exp_count = lax.axis_size("exp")
+    slots_dev = slot_count // exp_count
+    sums = sums.reshape(exp_count, slots_dev, plane_size + 128)
+    parts = lax.all_to_all(sums, "exp", split_axis=0, concat_axis=0, tiled=True)
+    totals = jnp.sum(parts.astype(jnp.float32), axis=0)
+    numerator = totals[:, :plane_size].reshape(slots_dev * tile_rows, tile_cols)
+    weight_sum = spread_cells(totals[:, plane_size : plane_size + 32], tile_rows, tile_cols)
+    return numerator / jnp.maximum(weight_sum.reshape(slots_dev * tile_rows, tile_cols), 1.0)
 
 
 def solution(mesh):

time: 194 us -> 92.6 us (0.48)
  the two profiles are of different devices: /device:TPU:2 before, /device:TPU:7 now
where the time goes in v1:
time: 92.6 us; the launch traced here: 92 us
  blocking collectives  53.2 us (57%)
  local copies, waits for them, and re-layouts  17.2 us (19%)
  matrix products  16.6 us (18%)
  other arithmetic  4.43 us (5%)
    all_to_all x1, blocking collectives, body(): recv = lax.all_to_all(send, 'sky', split_axis=0, concat_axis=0, tiled=True)  37.6 us
    all_to_all x1, blocking collectives, body(): parts = lax.all_to_all(sums, 'exp', split_axis=0, concat_axis=0, tiled=True)  15.6 us
    dot_general x6, matrix products, match_and_warp(): jnp.einsum('nij,nkj->nik', halfway, col_warp, preferred_element_type=jnp....  8.12 us
    dot_general x6, matrix products, match_and_warp(): jnp.einsum('nbij,bjk->nik', scaled, col_toeplitz, preferred_element_type=...  6.76 us
    dynamic_slice x12, local copies, waits for them, and re-layouts, body(): lax.map(match_and_warp, grouped).reshape(tiles_dev, tile_rows * tile_cols)  5.67 us
    reshape x6, local copies, waits for them, and re-layouts, match_and_warp(): padded.reshape(per_block, tile_rows + kernel_len - 1, tile_cols + kernel_...  4.5 us
    squeeze x12, local copies, waits for them, and re-layouts, body(): lax.map(match_and_warp, grouped).reshape(tiles_dev, tile_rows * tile_cols)  4.3 us

profile of v1, /device:TPU:7, one launch (start us, length us, event | category | flops | bytes accessed | tf_op | source)
XLA Modules:
  0.0 92.0 jit_solution(8557941766505794341)
XLA Ops:
  0.7 0.7 multiply_convert_fusion.1
  1.4 0.7 convert_multiply_fusion
  2.8 1.0 %fusion.126 = bf16[20,168,128]{2,0,1:T(8,128)(2,1)S(1)} fusion(s32[168,128]{1,0:T(8,128)S(1)} %iota_subtract_fusion.2, bf16[20,41]{1,0:T(8,128)(2,1)S(1)} %copy-done), kind=kOutput, calls=%fused_computation.110 | convolution fusion | flops 36578304 | bytes 947816 | tf_op jit(solution)/shard_map/xyk,bk->bxy/dot_general | solution.py:14
  4.5 30.8 %while.13 = (s32[]{:T(128)}, bf16[6,8,24,128]{3,2,1,0:T(8,128)(2,1)S(1)}, s32[6,8,2]{1,0,2:T(8,128)S(1)}, bf16[6,8,6,24]{3,1,0,2:T(8,128)(2,1)S(1)}, bf16[6,8,10...) while((s32[]{:T(128)}, ...), condition=%wide.region_3.4_spmd, body=%wide.region_2.3_spmd.sunk | while | flops 259956800 | bytes 2027581 | solution.py:97
  4.5 1.0 %constant_dynamic-slice_fusion.4 = bf16[1,8,10752]{2,1,0:T(8,128)(2,1)S(1)} fusion(bf16[6,8,10752]{2,1,0:T(8,128)(2,1)} %get-tuple-element.309, s32[]{:T(128)} %get-tuple-element.295), kind=kLoop, calls=%fused_computation.94.clone.1 | loop fusion | bytes 344068 | tf_op jit(solution)/shard_map/while/body/jit(dynamic_index_in_dim)/dynamic_slice | solution.py:97
  5.4 0.7 reshape.211
  6.2 1.1 %fusion.154 = bf16[8,24,128]{2,1,0:T(8,128)(2,1)S(1)} fusion(f32[8,20]{1,0:T(8,128)S(1)} %dynamic-slice_bitcast_fusion.6, bf16[20,168,128]{2,1,0:T(8,128)(2,1)S(1)} %get-tuple-element.312, bf16[8,64,168,1]{2,1,0,3:T(8,128)(2,1)S(1)} %reshape.211, bf16[20,24,64]{2,1,0:T(8,128)(2,1)S(1)} %get-tuple-element.310), kind=kOutput, calls=%fused_computation.4.clone.1 | convolution fusion | flops 249040896 | bytes 1143424 | tf_op jit(solution)/shard_map/while/body/eval_jaxpr/nbij,bjk->nik/dot_general | solution.py:83
  7.3 0.7 dynamic-slice_bitcast_fusion.7
  8.2 1.4 %fusion.155 = bf16[6,8,24,128]{3,2,1,0:T(8,128)(2,1)S(1)} fusion(bf16[6,8,24,128]{3,2,1,0:T(8,128)(2,1)S(1)} %get-tuple-element.296, s32[]{:T(128)} %get-tuple-element.295, bf16[8,24,128]{2,1,0:T(8,128)(2,1)S(1)} %fusion.154, s32[8,128]{1,0:T(8,128)S(1)} %add_clamp_fusion.4, bf16[8,128]{1,0:T(8,128)(2,1)S(1)} %get-tuple-element.272, ...), kind=kOutput, calls=%fused_computation.8.clone.1 | convolution fusion | flops 10912256 | bytes 131076 | tf_op jit(solution)/shard_map/while/body/eval_jaxpr/nij,nkj->nik/dot_general | solution.py:91
  9.6 0.9 %constant_dynamic-slice_fusion.4 = bf16[1,8,10752]{2,1,0:T(8,128)(2,1)S(1)} fusion(bf16[6,8,10752]{2,1,0:T(8,128)(2,1)} %get-tuple-element.309, s32[]{:T(128)} %get-tuple-element.295), kind=kLoop, calls=%fused_computation.94.clone.1 | loop fusion | bytes 344068 | tf_op jit(solution)/shard_map/while/body/jit(dynamic_index_in_dim)/dynamic_slice | solution.py:97
  10.5 0.7 reshape.211
  11.3 1.1 %fusion.154 = bf16[8,24,128]{2,1,0:T(8,128)(2,1)S(1)} fusion(f32[8,20]{1,0:T(8,128)S(1)} %dynamic-slice_bitcast_fusion.6, bf16[20,168,128]{2,1,0:T(8,128)(2,1)S(1)} %get-tuple-element.312, bf16[8,64,168,1]{2,1,0,3:T(8,128)(2,1)S(1)} %reshape.211, bf16[20,24,64]{2,1,0:T(8,128)(2,1)S(1)} %get-tuple-element.310), kind=kOutput, calls=%fused_computation.4.clone.1 | convolution fusion | flops 249040896 | bytes 1143424 | tf_op jit(solution)/shard_map/while/body/eval_jaxpr/nbij,bjk->nik/dot_general | solution.py:83
  12.4 0.7 dynamic-slice_bitcast_fusion.7
  13.4 1.4 %fusion.155 = bf16[6,8,24,128]{3,2,1,0:T(8,128)(2,1)S(1)} fusion(bf16[6,8,24,128]{3,2,1,0:T(8,128)(2,1)S(1)} %get-tuple-element.296, s32[]{:T(128)} %get-tuple-element.295, bf16[8,24,128]{2,1,0:T(8,128)(2,1)S(1)} %fusion.154, s32[8,128]{1,0:T(8,128)S(1)} %add_clamp_fusion.4, bf16[8,128]{1,0:T(8,128)(2,1)S(1)} %get-tuple-element.272, ...), kind=kOutput, calls=%fused_computation.8.clone.1 | convolution fusion | flops 10912256 | bytes 131076 | tf_op jit(solution)/shard_map/while/body/eval_jaxpr/nij,nkj->nik/dot_general | solution.py:91
  14.7 0.9 %constant_dynamic-slice_fusion.4 = bf16[1,8,10752]{2,1,0:T(8,128)(2,1)S(1)} fusion(bf16[6,8,10752]{2,1,0:T(8,128)(2,1)} %get-tuple-element.309, s32[]{:T(128)} %get-tuple-element.295), kind=kLoop, calls=%fused_computation.94.clone.1 | loop fusion | bytes 344068 | tf_op jit(solution)/shard_map/while/body/jit(dynamic_index_in_dim)/dynamic_slice | solution.py:97
  15.7 0.7 reshape.211
  16.4 1.1 %fusion.154 = bf16[8,24,128]{2,1,0:T(8,128)(2,1)S(1)} fusion(f32[8,20]{1,0:T(8,128)S(1)} %dynamic-slice_bitcast_fusion.6, bf16[20,168,128]{2,1,0:T(8,128)(2,1)S(1)} %get-tuple-element.312, bf16[8,64,168,1]{2,1,0,3:T(8,128)(2,1)S(1)} %reshape.211, bf16[20,24,64]{2,1,0:T(8,128)(2,1)S(1)} %get-tuple-element.310), kind=kOutput, calls=%fused_computation.4.clone.1 | convolution fusion | flops 249040896 | bytes 1143424 | tf_op jit(solution)/shard_map/while/body/eval_jaxpr/nbij,bjk->nik/dot_general | solution.py:83
  18.5 1.4 %fusion.155 = bf16[6,8,24,128]{3,2,1,0:T(8,128)(2,1)S(1)} fusion(bf16[6,8,24,128]{3,2,1,0:T(8,128)(2,1)S(1)} %get-tuple-element.296, s32[]{:T(128)} %get-tuple-element.295, bf16[8,24,128]{2,1,0:T(8,128)(2,1)S(1)} %fusion.154, s32[8,128]{1,0:T(8,128)S(1)} %add_clamp_fusion.4, bf16[8,128]{1,0:T(8,128)(2,1)S(1)} %get-tuple-element.272, ...), kind=kOutput, calls=%fused_computation.8.clone.1 | convolution fusion | flops 10912256 | bytes 131076 | tf_op jit(solution)/shard_map/while/body/eval_jaxpr/nij,nkj->nik/dot_general | solution.py:91
  19.9 0.9 %constant_dynamic-slice_fusion.4 = bf16[1,8,10752]{2,1,0:T(8,128)(2,1)S(1)} fusion(bf16[6,8,10752]{2,1,0:T(8,128)(2,1)} %get-tuple-element.309, s32[]{:T(128)} %get-tuple-element.295), kind=kLoop, calls=%fused_computation.94.clone.1 | loop fusion | bytes 344068 | tf_op jit(solution)/shard_map/while/body/jit(dynamic_index_in_dim)/dynamic_slice | solution.py:97
  20.8 0.7 reshape.211
  21.6 1.1 %fusion.154 = bf16[8,24,128]{2,1,0:T(8,128)(2,1)S(1)} fusion(f32[8,20]{1,0:T(8,128)S(1)} %dynamic-slice_bitcast_fusion.6, bf16[20,168,128]{2,1,0:T(8,128)(2,1)S(1)} %get-tuple-element.312, bf16[8,64,168,1]{2,1,0,3:T(8,128)(2,1)S(1)} %reshape.211, bf16[20,24,64]{2,1,0:T(8,128)(2,1)S(1)} %get-tuple-element.310), kind=kOutput, calls=%fused_computation.4.clone.1 | convolution fusion | flops 249040896 | bytes 1143424 | tf_op jit(solution)/shard_map/while/body/eval_jaxpr/nbij,bjk->nik/dot_general | solution.py:83
  23.6 1.4 %fusion.155 = bf16[6,8,24,128]{3,2,1,0:T(8,128)(2,1)S(1)} fusion(bf16[6,8,24,128]{3,2,1,0:T(8,128)(2,1)S(1)} %get-tuple-element.296, s32[]{:T(128)} %get-tuple-element.295, bf16[8,24,128]{2,1,0:T(8,128)(2,1)S(1)} %fusion.154, s32[8,128]{1,0:T(8,128)S(1)} %add_clamp_fusion.4, bf16[8,128]{1,0:T(8,128)(2,1)S(1)} %get-tuple-element.272, ...), kind=kOutput, calls=%fused_computation.8.clone.1 | convolution fusion | flops 10912256 | bytes 131076 | tf_op jit(solution)/shard_map/while/body/eval_jaxpr/nij,nkj->nik/dot_general | solution.py:91
  25.0 0.9 %constant_dynamic-slice_fusion.4 = bf16[1,8,10752]{2,1,0:T(8,128)(2,1)S(1)} fusion(bf16[6,8,10752]{2,1,0:T(8,128)(2,1)} %get-tuple-element.309, s32[]{:T(128)} %get-tuple-element.295), kind=kLoop, calls=%fused_computation.94.clone.1 | loop fusion | bytes 344068 | tf_op jit(solution)/shard_map/while/body/jit(dynamic_index_in_dim)/dynamic_slice | solution.py:97
  25.9 0.7 reshape.211
  26.7 1.1 %fusion.154 = bf16[8,24,128]{2,1,0:T(8,128)(2,1)S(1)} fusion(f32[8,20]{1,0:T(8,128)S(1)} %dynamic-slice_bitcast_fusion.6, bf16[20,168,128]{2,1,0:T(8,128)(2,1)S(1)} %get-tuple-element.312, bf16[8,64,168,1]{2,1,0,3:T(8,128)(2,1)S(1)} %reshape.211, bf16[20,24,64]{2,1,0:T(8,128)(2,1)S(1)} %get-tuple-element.310), kind=kOutput, calls=%fused_computation.4.clone.1 | convolution fusion | flops 249040896 | bytes 1143424 | tf_op jit(solution)/shard_map/while/body/eval_jaxpr/nbij,bjk->nik/dot_general | solution.py:83
  28.7 1.4 %fusion.155 = bf16[6,8,24,128]{3,2,1,0:T(8,128)(2,1)S(1)} fusion(bf16[6,8,24,128]{3,2,1,0:T(8,128)(2,1)S(1)} %get-tuple-element.296, s32[]{:T(128)} %get-tuple-element.295, bf16[8,24,128]{2,1,0:T(8,128)(2,1)S(1)} %fusion.154, s32[8,128]{1,0:T(8,128)S(1)} %add_clamp_fusion.4, bf16[8,128]{1,0:T(8,128)(2,1)S(1)} %get-tuple-element.272, ...), kind=kOutput, calls=%fused_computation.8.clone.1 | convolution fusion | flops 10912256 | bytes 131076 | tf_op jit(solution)/shard_map/while/body/eval_jaxpr/nij,nkj->nik/dot_general | solution.py:91
  30.1 0.9 %constant_dynamic-slice_fusion.4 = bf16[1,8,10752]{2,1,0:T(8,128)(2,1)S(1)} fusion(bf16[6,8,10752]{2,1,0:T(8,128)(2,1)} %get-tuple-element.309, s32[]{:T(128)} %get-tuple-element.295), kind=kLoop, calls=%fused_computation.94.clone.1 | loop fusion | bytes 344068 | tf_op jit(solution)/shard_map/while/body/jit(dynamic_index_in_dim)/dynamic_slice | solution.py:97
  31.1 0.7 reshape.211
  31.8 1.1 %fusion.154 = bf16[8,24,128]{2,1,0:T(8,128)(2,1)S(1)} fusion(f32[8,20]{1,0:T(8,128)S(1)} %dynamic-slice_bitcast_fusion.6, bf16[20,168,128]{2,1,0:T(8,128)(2,1)S(1)} %get-tuple-element.312, bf16[8,64,168,1]{2,1,0,3:T(8,128)(2,1)S(1)} %reshape.211, bf16[20,24,64]{2,1,0:T(8,128)(2,1)S(1)} %get-tuple-element.310), kind=kOutput, calls=%fused_computation.4.clone.1 | convolution fusion | flops 249040896 | bytes 1143424 | tf_op jit(solution)/shard_map/while/body/eval_jaxpr/nbij,bjk->nik/dot_general | solution.py:83
  33.9 1.4 %fusion.155 = bf16[6,8,24,128]{3,2,1,0:T(8,128)(2,1)S(1)} fusion(bf16[6,8,24,128]{3,2,1,0:T(8,128)(2,1)S(1)} %get-tuple-element.296, s32[]{:T(128)} %get-tuple-element.295, bf16[8,24,128]{2,1,0:T(8,128)(2,1)S(1)} %fusion.154, s32[8,128]{1,0:T(8,128)S(1)} %add_clamp_fusion.4, bf16[8,128]{1,0:T(8,128)(2,1)S(1)} %get-tuple-element.272, ...), kind=kOutput, calls=%fused_computation.8.clone.1 | convolution fusion | flops 10912256 | bytes 131076 | tf_op jit(solution)/shard_map/while/body/eval_jaxpr/nij,nkj->nik/dot_general | solution.py:91
  36.7 37.6 %all_to_all.10 = bf16[64,2,3200]{2,1,0:T(2,128)(2,1)S(1)} all-to-all(bf16[64,2,3200]{2,1,0:T(2,128)(2,1)S(1)} %reshape.196), channel_id=1, replica_groups=mesh['sky'=64,'exp'=8] {'sky'}, dimensions={0} | all-to-all | bytes 1638400 | tf_op jit(solution)/shard_map/all_to_all | solution.py:125
  75.1 15.6 %all_to_all.11 = bf16[8,2,3200]{2,1,0:T(2,128)(2,1)S(1)} all-to-all(bf16[8,2,3200]{2,1,0:T(2,128)(2,1)S(1)} %reshape.198), channel_id=1, replica_groups=mesh['sky'=64,'exp'=8] {'exp'}, dimensions={0} | all-to-all | bytes 204800 | tf_op jit(solution)/shard_map/all_to_all | solution.py:135
  (109 shorter events, 9.4 us)
Async XLA Ops:
  0.0 2.8 %copy-start = (bf16[20,41]{1,0:T(8,128)(2,1)S(1)}, bf16[20,41]{1,0:T(8,128)(2,1)}, u32[]{:S(2)}) copy-start(bf16[20,41]{1,0:T(8,128)(2,1)} %param.23) | copy-start | bytes 4924
  2.8 1.1 %copy-start.5 = (bf16[20,41]{1,0:T(8,128)(2,1)S(1)}, bf16[20,41]{1,0:T(8,128)(2,1)}, u32[]{:S(2)}) copy-start(bf16[20,41]{1,0:T(8,128)(2,1)} %param.22) | copy-start | bytes 4924
  2.8 1.4 %copy-start.1 = (bf16[48,6,24]{0,2,1:T(8,128)(2,1)S(1)}, bf16[48,6,24]{0,2,1:T(8,128)(2,1)}, u32[]{:S(2)}) copy-start(bf16[48,6,24]{0,2,1:T(8,128)(2,1)} %param.15) | copy-start | bytes 41476
  2.8 1.5 %copy-start.2 = (f32[48,20]{0,1:T(8,128)S(1)}, f32[48,20]{0,1:T(8,128)}, u32[]{:S(2)}) copy-start(f32[48,20]{0,1:T(8,128)} %param.14) | copy-start | bytes 11524
  2.8 1.6 %copy-start.4 = (s32[48,2]{0,1:T(2,128)S(1)}, s32[48,2]{0,1:T(2,128)}, u32[]{:S(2)}) copy-start(s32[48,2]{0,1:T(2,128)} %param.17) | copy-start | bytes 1156
  4.4 30.8 %copy-start.6 = (s32[48]{0:T(128)S(1)}, s32[48]{0:T(128)}, u32[]{:S(2)}) copy-start(s32[48]{0:T(128)} %param.21) | copy-start | bytes 580
  4.4 31.0 %copy-start.3 = (s32[48,1]{0,1:T(1,128)S(1)}, s32[48,1]{0,1:T(1,128)}, u32[]{:S(2)}) copy-start(s32[48,1]{0,1:T(1,128)} %param.20) | copy-start | bytes 580

commit v2 on v1

v2 whole, which is shorter than its diff:
```python
import jax
import jax.numpy as jnp
from jax import lax
from jax.experimental import pallas as pl
from jax.experimental.pallas import tpu as pltpu
from jax.sharding import PartitionSpec as P
F32 = jnp.float32
BF16 = jnp.bfloat16
TRIOS = 16
NB = 20
KW = 41
TR = 24
TC = 128
IR = TR + KW - 1
IC = TC + KW - 1
SPAN = 5


def iota(shape, axis):
    return lax.broadcasted_iota(jnp.int32, shape, axis)


def unpack_tiles(tiles_ref, flat, image):
    for octet in range(6):
        for p in range(84):
            block = tiles_ref[pl.ds(8 * octet, 8), pl.ds(128 * p, 128)].astype(F32)
            flat[pl.ds(8 * octet * 84 + p, 8, stride=84), :] = block
    lane = iota((64, 128), 1)
    for m in range(16):
        first, rest = divmod(IC * m, 128)
        parts = [None] * 4
        for third in range(3):
            shift = (rest - IC * third) % 128
            base = third * 16 * 84 + first
            rolled = {}

            def row(q, rolled=rolled, base=base, shift=shift):
                if q not in rolled:
                    val = flat[pl.ds(base + q, 64, stride=21), :]
                    rolled[q] = pltpu.roll(val, (128 - shift) % 128, 1) if shift else val
                return rolled[q]

            for d in range(4):
                lo, hi = max(128 * d, IC * third), min(128 * d + 128, IC * third + IC)
                if lo >= hi:
                    continue
                start = rest - IC * third + 128 * d
                q0 = start // 128
                edge = 128 - start % 128
                l0, l1 = lo - 128 * d, hi - 128 * d
                if l1 <= edge:
                    val = row(q0)
                elif l0 >= edge:
                    val = row(q0 + 1)
                else:
                    val = jnp.where(lane < edge, row(q0), row(q0 + 1))
                if parts[d] is None:
                    parts[d] = val if l1 == 128 else jnp.where(lane < l1, val, 0.0)
                else:
                    parts[d] = jnp.where(lane < l0, parts[d], val if l1 == 128 else jnp.where(lane < l1, val, 0.0))
        for d in range(4):
            image[pl.ds(d * TRIOS * IR + m, 64, stride=16), :] = parts[d]


def make_tables(brow_ref, bcol_ref, pad, rtab, w0, w1):
    pad[...] = jnp.zeros((32, 128), F32)
    pad[0:NB, 0:KW] = brow_ref[...].astype(F32)
    for b in range(NB):
        line = jnp.broadcast_to(pad[pl.ds(b, 1), :], (TR, 128))
        line = pltpu.roll(line, 0, 1, stride=1, stride_axis=0)
        rtab[pl.ds(b * TR, TR), :] = line
    pad[0:NB, 0:KW] = bcol_ref[...].astype(F32)
    mirror = ((iota((128, 128), 0) + iota((128, 128), 1)) % 128 == 0).astype(BF16)
    rev = jnp.dot(pad[...].astype(BF16), mirror, preferred_element_type=F32)
    pad[...] = rev
    gap = iota((IC, 128), 0) - iota((IC, 128), 1)
    inside = (gap >= 0) & (gap < KW)
    for b in range(NB):
        line = jnp.broadcast_to(pad[pl.ds(b, 1), :], (128, 128))
        line = pltpu.roll(line, 0, 1, stride=1, stride_axis=0)
        band = jnp.concatenate([line, line[: IC - 128]], axis=0)
        band = jnp.where(inside, band, 0.0)
        zero = jnp.zeros((176, 128), F32)
        r = pl.ds(b * 256, 256)
        w0[r, 0:128] = jnp.concatenate([band, zero[:88]], axis=0).astype(BF16)
        w0[r, 128:256] = jnp.concatenate([zero[:168], band[:88]], axis=0).astype(BF16)
        w1[r, 0:128] = jnp.concatenate([band[88:168], zero[:176]], axis=0).astype(BF16)
        w1[r, 128:256] = jnp.concatenate([zero[:80], band, zero[:8]], axis=0).astype(BF16)


def row_stage(image, rtab, coef_s, s0, s1):
    table = rtab[...].astype(BF16)[:, :IR]
    lane = iota((8, 512), 1)

    def step(u, carry):
        halves = []
        for h in range(2):
            n = 2 * u + h
            x = jnp.concatenate(
                [image[pl.ds(pl.multiple_of(d * TRIOS * IR + n * IR, 8), IR), :] for d in range(4)],
                axis=1,
            ).astype(BF16)
            halves.append((n, jnp.dot(table, x, preferred_element_type=F32)))
        for b in range(NB):
            rows = []
            for n, rp in halves:
                scale = jnp.where(
                    lane < IC,
                    coef_s[n, b],
                    jnp.where(lane < 2 * IC, coef_s[n + 16, b], coef_s[n + 32, b]),
                )
                for a in range(3):
                    k = b * TR + 8 * a
                    rows.append(rp[k : k + 8] * scale)
            block = jnp.concatenate(rows, axis=0).astype(BF16)
            at = pl.ds(pl.multiple_of(48 * u, 16), 48)
            s0[at, pl.ds(b * 256, 256)] = block[:, :256]
            s1[at, pl.ds(b * 256, 256)] = block[:, 256:]
        return carry

    lax.fori_loop(0, TRIOS // 2, step, 0)


def column_weights(ctap_ref, shiftv_ref, taps, diag):
    for t in range(48):
        taps[pl.ds(8 * t, 6), :] = ctap_ref[t].astype(F32)
    j = iota((48, 128), 1)
    shift = jnp.broadcast_to(shiftv_ref[:, 1:2], (48, 128))
    offset = jnp.clip(j + shift - 3, 0, TC - 6) - j
    kept = [taps[pl.ds(k, 48, stride=8), :] for k in range(6)]
    for o in range(-SPAN, SPAN + 1):
        total = jnp.zeros((48, 128), F32)
        for k in range(6):
            total = jnp.where(offset + k == o, kept[k], total)
        diag[o + SPAN] = total


def row_weights(rtap_ref, taps):
    taps[...] = jnp.zeros(taps.shape, F32)
    for third in range(3):
        for n in range(TRIOS):
            taps[pl.ds(8 * n, 6), pl.ds(TR * third, TR)] = rtap_ref[n + 16 * third].astype(F32)


def warp_stage(p0, p1, shifts_s, words_s, weights_s, dest_s, slot_s, rowtaps, diag, count, out_ref):
    out_ref[...] = jnp.zeros(out_ref.shape, BF16)

    def clear(d, carry):
        count[d] = 0
        return carry

    lax.fori_loop(0, 64, clear, 0)
    bit = 8 * (iota((TR, 128), 0) // 6) + iota((TR, 128), 1) // 16
    lane8, sub8 = iota((8, 128), 1), iota((8, 128), 0)
    lane1 = iota((1, 128), 1)
    third_of, row_of = lane1 // TR, lane1 % TR
    rr = iota((72, 128), 0)

    def trio(n, carry):
        at = pl.ds(pl.multiple_of(n * TR, 8), TR)
        left, right = p0[at, :], p1[at, :]
        stack = jnp.concatenate(
            [left[:, :128], left[:, 128:] + right[:, :128], right[:, 128:]], axis=0
        ).astype(BF16)
        shift = jnp.where(
            third_of == 0,
            shifts_s[n, 0],
            jnp.where(third_of == 1, shifts_s[n + 16, 0], shifts_s[n + 32, 0]),
        )
        base = third_of * TR + jnp.clip(row_of + shift - 3, 0, TR - 6)
        delta = rr - jnp.broadcast_to(base, (72, 128))
        taps = rowtaps[pl.ds(pl.multiple_of(8 * n, 8), 8), :]
        band = jnp.zeros((72, 128), F32)
        for k in range(6):
            band = jnp.where(delta == k, jnp.broadcast_to(taps[k : k + 1], (72, 128)), band)
        half = lax.dot_general(
            band.astype(BF16), stack, (((0,), (0,)), ((), ())), preferred_element_type=F32
        )
        for third in range(3):
            t = n + 16 * third
            h = half[TR * third : TR * third + TR]
            acc = jnp.zeros((TR, 128), F32)
            for o in range(-SPAN, SPAN + 1):
                d = diag[o + SPAN, pl.ds(t, 1), :]
                moved = pltpu.roll(h, (-o) % 128, 1) if o else h
                acc = acc + jnp.broadcast_to(d, (TR, 128)) * moved
            word, weight = words_s[t], weights_s[t]
            flagged = lax.shift_right_logical(jnp.full((TR, 128), word, jnp.int32), bit) & 1
            prod = (acc * jnp.where(flagged == 0, weight, 0.0)).astype(BF16)
            to = dest_s[t, 0]
            rank = count[to]
            count[to] = rank + 1
            for a in range(3):
                out_ref[to, 3 * rank + a] = prod[8 * a : 8 * a + 8]
            flag8 = lax.shift_right_logical(jnp.full((8, 128), word, jnp.int32), lane8 & 31) & 1
            head = jnp.where(
                lane8 < 32,
                jnp.where(flag8 == 0, weight, 0.0),
                jnp.where(lane8 == 32, jnp.full((8, 128), slot_s[t], jnp.int32).astype(F32), 0.0),
            )
            old = out_ref[to, 6].astype(F32)
            out_ref[to, 6] = jnp.where(sub8 == rank, head, old).astype(BF16)
        return carry

    lax.fori_loop(0, TRIOS, trio, 0)


def send_kernel(
    words_s,
    weights_s,
    dest_s,
    slot_s,
    shifts_s,
    coef_s,
    shiftv_ref,
    tiles_ref,
    rtap_ref,
    ctap_ref,
    brow_ref,
    bcol_ref,
    out_ref,
    flat,
    image,
    pad,
    rtab,
    w0,
    w1,
    s0,
    s1,
    p0,
    p1,
    taps,
    rowtaps,
    diag,
    count,
):
    unpack_tiles(tiles_ref, flat, image)
    make_tables(brow_ref, bcol_ref, pad, rtab, w0, w1)
    column_weights(ctap_ref, shiftv_ref, taps, diag)
    row_weights(rtap_ref, rowtaps)
    row_stage(image, rtab, coef_s, s0, s1)
    p0[...] = jnp.dot(s0[...], w0[...], preferred_element_type=F32)
    p1[...] = jnp.dot(s1[...], w1[...], preferred_element_type=F32)
    warp_stage(
        p0, p1, shifts_s, words_s, weights_s, dest_s, slot_s, rowtaps, diag, count, out_ref
    )


def send_blocks(tiles, coef, rtap, ctap, shifts, words, weights, dest, slot, brow, bcol):
    smem = pl.BlockSpec(memory_space=pltpu.SMEM)
    vmem = pl.BlockSpec(memory_space=pltpu.VMEM)
    return pl.pallas_call(
        send_kernel,
        out_shape=jax.ShapeDtypeStruct((64, 7, 8, 128), BF16),
        in_specs=[smem] * 6 + [vmem] * 6,
        out_specs=vmem,
        scratch_shapes=[
            pltpu.VMEM((48 * 84 + 8, 128), F32),
            pltpu.VMEM((4 * TRIOS * IR, 128), F32),
            pltpu.VMEM((32, 128), F32),
            pltpu.VMEM((NB * TR, 128), F32),
            pltpu.VMEM((NB * 256, 256), BF16),
            pltpu.VMEM((NB * 256, 256), BF16),
            pltpu.VMEM((384, NB * 256), BF16),
            pltpu.VMEM((384, NB * 256), BF16),
            pltpu.VMEM((384, 256), F32),
            pltpu.VMEM((384, 256), F32),
            pltpu.VMEM((48 * 8, 128), F32),
            pltpu.VMEM((TRIOS * 8, 128), F32),
            pltpu.VMEM((2 * SPAN + 1, 48, 128), F32),
            pltpu.SMEM((64,), jnp.int32),
        ],
        compiler_params=pltpu.CompilerParams(vmem_limit_bytes=50 << 20),
        name="match_and_warp",
    )(words, weights.astype(F32), dest, slot, shifts, coef, shifts, tiles, rtap, ctap, brow, bcol)


def body(
    padded_tiles,
    coefficients,
    row_taps,
    col_taps,
    shifts,
    mask_words,
    weights,
    destination,
    patch_slot,
    basis_rows,
    basis_cols,
):
    send = send_blocks(
        padded_tiles,
        coefficients,
        row_taps,
        col_taps,
        shifts,
        mask_words,
        weights,
        destination,
        patch_slot,
        basis_rows,
        basis_cols,
    ).reshape(64, 56, 128)
    recv = lax.all_to_all(send, "sky", split_axis=0, concat_axis=0, tiled=True)
    planes = recv[:, :48].reshape(128, TR * TC)
    heads = recv[:, 48:50].reshape(128, 128)
    slot_of = heads[:, 32].astype(jnp.int32)
    pick = (iota((16, 128), 0) == slot_of[None, :]).astype(BF16)
    sums = jnp.dot(pick, planes, preferred_element_type=F32).astype(BF16)
    cells = jnp.dot(pick, heads, preferred_element_type=F32).astype(BF16)
    parts = jnp.concatenate(
        [sums.reshape(8, 48, 128), cells.reshape(8, 2, 128), jnp.zeros((8, 6, 128), BF16)], axis=1
    )
    parts = lax.all_to_all(parts, "exp", split_axis=0, concat_axis=0, tiled=True)
    totals = jnp.sum(parts.astype(F32), axis=0)
    weight_sum = spread_cells(totals[48:50, :32]).reshape(48, 128)
    return totals[:48] / jnp.maximum(weight_sum, 1.0)


def spread_cells(cells):
    grid = jnp.repeat(cells.reshape(2, 4, 8), TR // 4, axis=1)
    return jnp.repeat(grid, TC // 8, axis=2)


def solution(mesh):
    placed = (
        P(("sky", "exp"), None),
        P(("sky", "exp"), None),
        P(("sky", "exp"), None, None),
        P(("sky", "exp"), None, None),
        P(("sky", "exp"), None),
        P(("sky", "exp")),
        P(("sky", "exp")),
        P(("sky", "exp"), None),
        P(("sky", "exp")),
        P(),
        P(),
    )
    return jax.shard_map(
        body, mesh=mesh, in_specs=placed, out_specs=P(("sky", "exp"), None), check_vma=False
    )
```

time: 92.6 us -> 80.3 us (0.87)
  blocking collectives: 53.2 us -> 15.5 us
  waiting for transfers between devices: 0 us -> 25.5 us
  Pallas kernels: 0 us -> 16.6 us
  matrix products: 16.6 us -> 0.34 us
  starting transfers between devices: 0 us -> 14.3 us
  local copies, waits for them, and re-layouts: 17.2 us -> 6.61 us
  other arithmetic: 4.43 us -> 0.94 us
    all_to_all x2 -> x1, blocking collectives: 53.2 us -> 15.5 us  [body(): lax.all_to_all(parts, 'exp', split_axis=0, concat_axis=0, tiled=True)]
    all_to_all x0 -> x1, waiting for transfers between devices: none -> 25.5 us  [body(): recv = lax.all_to_all(send, 'sky', split_axis=0, concat_axis=0, tiled=True)]
    pallas_call x0 -> x1, Pallas kernels: none -> 16.6 us  [send_blocks(): pl.pallas_call(send_kernel, out_shape=jax.ShapeDtypeStruct((64, 7, 8, 128...]
    dot_general x16 -> x2, matrix products: 16.6 us -> 0.34 us  [the longest x1 0.21 us: body(): sums = jnp.dot(pick, planes, preferred_element_type=F32).astype(BF16)]
    all_to_all x0 -> x1, starting transfers between devices: none -> 14.3 us  [body(): recv = lax.all_to_all(send, 'sky', split_axis=0, concat_axis=0, tiled=True)]
    dynamic_slice x12 -> x0, local copies, waits for them, and re-layouts: 5.67 us -> none  [body(): lax.map(match_and_warp, grouped).reshape(tiles_dev, tile_rows * tile_cols)]
    reshape x12 -> x2, local copies, waits for them, and re-layouts: 5.73 us -> 0.39 us  [the longest x1 0.33 us: body(): planes = recv[:, :48].reshape(128, TR * TC)]
    unnamed x16 -> x25, local copies, waits for them, and re-layouts: 0.24 us -> 5.48 us
  transfers between devices with their start and end apart: 0 -> 1, of which waited for: 0 -> 1; matrix products, arithmetic and copies ran while one was open for 0% -> 0% of each run, Pallas kernels for 0% -> 0%
where the time goes in v2:
time: 80.3 us; the launch traced here: 79.9 us
  waiting for transfers between devices  25.5 us (32%)
  Pallas kernels  16.6 us (21%)
  blocking collectives  15.5 us (19%)
  starting transfers between devices  14.3 us (18%)
  local copies, waits for them, and re-layouts  6.61 us (8%)
  other arithmetic  0.94 us (1%)
    all_to_all x1, waiting for transfers between devices, body(): recv = lax.all_to_all(send, 'sky', split_axis=0, concat_axis=0, tiled=True)  25.5 us
    pallas_call x1, Pallas kernels, send_blocks(): pl.pallas_call(send_kernel, out_shape=jax.ShapeDtypeStruct((64, 7, 8, 128...  16.6 us
    all_to_all x1, blocking collectives, body(): lax.all_to_all(parts, 'exp', split_axis=0, concat_axis=0, tiled=True)  15.5 us
    all_to_all x1, starting transfers between devices, body(): recv = lax.all_to_all(send, 'sky', split_axis=0, concat_axis=0, tiled=True)  14.3 us
    unnamed x25, local copies, waits for them, and re-layouts  5.48 us
  transfers between devices with their start and end apart: 1, of which 1 were waited for; matrix products, arithmetic and copies ran while one was open for 0% of the time, Pallas kernels for 0%

profile of v2, /device:TPU:7, one launch (start us, length us, event | category | flops | bytes accessed | tf_op | source)
XLA Modules:
  0.0 79.9 jit_solution(18302231657113335478)
XLA Ops:
  0.0 0.9 %copy.43.rtap_ref = bf16[48,6,24]{2,1,0:T(8,128)(2,1)S(1)} copy(bf16[48,6,24]{0,2,1:T(8,128)(2,1)} %param.13) | data formatting | bytes 27648 | tf_op args[2]
  1.0 0.6 copy-done.8
  1.6 0.1 copy.39.dest_s
  1.7 0.6 copy-done.7
  2.3 0.1 copy.40.shifts_s.shiftv_ref
  2.4 0.6 copy-done.6
  3.0 0.1 copy.41.coef_s
  3.1 0.6 copy-done.9
  3.6 0.0 copy-done.1
  3.7 0.0 copy-done.2
  3.7 0.6 copy-done.3
  4.3 0.0 copy-done.4
  4.3 1.2 %copy-done = bf16[48,10752]{1,0:T(8,128)(2,1)S(1)} copy-done((bf16[48,10752]{1,0:T(8,128)(2,1)S(1)}, bf16[48,10752]{1,0:T(8,128)(2,1)}, u32[]{:S(2)}) %copy-start) | copy-done | bytes 1032216
  5.5 16.6 %match_and_warp.1 = bf16[64,7,8,128]{3,2,1,0:T(8,128)(2,1)} custom-call(s32[48]{0:T(128)S(1)} %copy-done.3, f32[48]{0:T(128)S(1)} %convert_element_type.23.weights_s, s32[48,1]{1,0:T(8,128)S(1)} %copy.39.dest_s, s32[48]{0:T(128)S(1)} %copy-done.4, s32[48,2]{1,0:T(8,128)S(1)} %copy.40.shifts_s.shiftv_ref, f32[48,20]{1,0:T(8,128)S(1)} %copy.41.coef_s, ...), custom_call_target="tpu_custom_call" | custom-call | tf_op jit(solution)/shard_map/match_and_warp/pallas_call | solution.py:252
  22.2 14.3 %all-to-all-start = ((bf16[64,56,128]{2,1,0:T(8,128)(2,1)}), bf16[64,56,128]{2,1,0:T(8,128)(2,1)S(1)}, u32[]{:S(2)}, u32[]{:S(2)}) async-start(bf16[64,56,128]{2,1,0:T(8,128)(2,1)} %bitcast), calls=%async_computation | async-start | bytes 1835008 | tf_op jit(solution)/shard_map/all_to_all | solution.py:304
  36.5 0.1 pad.2.clone
  36.6 25.5 %all-to-all-done = bf16[64,56,128]{2,1,0:T(8,128)(2,1)S(1)} async-done(((bf16[64,56,128]{2,1,0:T(8,128)(2,1)}), bf16[64,56,128]{2,1,0:T(8,128)(2,1)S(1)}, u32[]{:S(2)}, u32[]{:S(2)}) %all-to-all-start) | async-done | bytes 917536 | tf_op jit(solution)/shard_map/all_to_all | solution.py:304
  62.1 0.2 convert_reduce_fusion.1
  62.3 0.1 convolution_convert_fusion.1
  62.4 0.1 slice.22
  62.5 0.3 reshape.32
  62.8 0.2 convolution_convert_fusion
  63.0 0.1 reshape.33
  63.1 0.1 maximum_maximum_fusion
  63.2 15.5 %all_to_all.10 = bf16[8,56,128]{2,1,0:T(8,128)(2,1)S(1)} all-to-all(bf16[8,56,128]{2,1,0:T(8,128)(2,1)S(1)} %maximum_maximum_fusion), channel_id=1, replica_groups=mesh['sky'=64,'exp'=8] {'exp'}, dimensions={0} | all-to-all | bytes 229376 | tf_op jit(solution)/shard_map/all_to_all | solution.py:314
  78.7 0.1 max.19
  78.8 0.1 copy.45
  78.9 0.1 broadcast_in_dim.11
  78.9 0.1 max.20
  79.1 0.1 max.21
  79.2 0.1 copy.47
  79.3 0.6 slice_divide_fusion
  (19 shorter events, 0.1 us)
Async XLA Ops:
  0.0 0.9 %copy-start.5 = (bf16[48,6,128]{2,0,1:T(8,128)(2,1)S(1)}, bf16[48,6,128]{2,0,1:T(8,128)(2,1)}, u32[]{:S(2)}) copy-start(bf16[48,6,128]{2,0,1:T(8,128)(2,1)} %param.14) | copy-start | bytes 221188
  0.9 0.7 copy-start.8
  1.6 0.7 copy-start.7
  2.3 0.7 copy-start.6
  3.0 0.7 copy-start.9
  3.0 0.7 copy-start.1
  3.0 0.7 copy-start.2
  3.6 0.7 copy-start.3
  3.6 0.7 copy-start.4
  4.3 1.2 %copy-start = (bf16[48,10752]{1,0:T(8,128)(2,1)S(1)}, bf16[48,10752]{1,0:T(8,128)(2,1)}, u32[]{:S(2)}) copy-start(bf16[48,10752]{1,0:T(8,128)(2,1)} %tiles_ref.1) | copy-start | bytes 3096580
  22.2 39.9 %all-to-all-start = ((bf16[64,56,128]{2,1,0:T(8,128)(2,1)}), bf16[64,56,128]{2,1,0:T(8,128)(2,1)S(1)}, u32[]{:S(2)}, u32[]{:S(2)}) async-start(bf16[64,56,128]{2,1,0:T(8,128)(2,1)} %bitcast), calls=%async_computation | async-start | bytes 1835008 | tf_op jit(solution)/shard_map/all_to_all | solution.py:304

commit v3 on v2

--- a/solution.py
+++ b/solution.py
@@ -4,6 +4,7 @@
 from jax.experimental import pallas as pl
 from jax.experimental.pallas import tpu as pltpu
 from jax.sharding import PartitionSpec as P
+
 F32 = jnp.float32
 BF16 = jnp.bfloat16
 TRIOS = 16
@@ -20,8 +21,9 @@
     return lax.broadcasted_iota(jnp.int32, shape, axis)
 
 
-def unpack_tiles(tiles_ref, flat, image):
+def unpack_tiles(tiles_ref, copies, flat, image):
     for octet in range(6):
+        copies[octet].wait()
         for p in range(84):
             block = tiles_ref[pl.ds(8 * octet, 8), pl.ds(128 * p, 128)].astype(F32)
             flat[pl.ds(8 * octet * 84 + p, 8, stride=84), :] = block
@@ -106,8 +108,8 @@
             for n, rp in halves:
                 scale = jnp.where(
                     lane < IC,
-                    coef_s[n, b],
-                    jnp.where(lane < 2 * IC, coef_s[n + 16, b], coef_s[n + 32, b]),
+                    coef_s[b, n],
+                    jnp.where(lane < 2 * IC, coef_s[b, n + 16], coef_s[b, n + 32]),
                 )
                 for a in range(3):
                     k = b * TR + 8 * a
@@ -121,13 +123,16 @@
     lax.fori_loop(0, TRIOS // 2, step, 0)
 
 
-def column_weights(ctap_ref, shiftv_ref, taps, diag):
-    for t in range(48):
-        taps[pl.ds(8 * t, 6), :] = ctap_ref[t].astype(F32)
+def column_weights(ctap_ref, shifts_ref, diag):
     j = iota((48, 128), 1)
-    shift = jnp.broadcast_to(shiftv_ref[:, 1:2], (48, 128))
-    offset = jnp.clip(j + shift - 3, 0, TC - 6) - j
-    kept = [taps[pl.ds(k, 48, stride=8), :] for k in range(6)]
+    own = jnp.where(
+        iota((48, 48), 0) == iota((48, 48), 1),
+        jnp.broadcast_to(shifts_ref[1:2, :], (48, 48)).astype(F32),
+        0.0,
+    )
+    shift = jnp.dot(own.astype(BF16), jnp.ones((48, 128), BF16), preferred_element_type=F32)
+    offset = jnp.clip(j + shift.astype(jnp.int32) - 3, 0, TC - 6) - j
+    kept = [ctap_ref[k].astype(F32) for k in range(6)]
     for o in range(-SPAN, SPAN + 1):
         total = jnp.zeros((48, 128), F32)
         for k in range(6):
@@ -135,23 +140,15 @@
         diag[o + SPAN] = total
 
 
-def row_weights(rtap_ref, taps):
-    taps[...] = jnp.zeros(taps.shape, F32)
-    for third in range(3):
-        for n in range(TRIOS):
-            taps[pl.ds(8 * n, 6), pl.ds(TR * third, TR)] = rtap_ref[n + 16 * third].astype(F32)
-
-
-def warp_stage(p0, p1, shifts_s, words_s, weights_s, dest_s, slot_s, rowtaps, diag, count, out_ref):
-    out_ref[...] = jnp.zeros(out_ref.shape, BF16)
-
-    def clear(d, carry):
-        count[d] = 0
-        return carry
-
-    lax.fori_loop(0, 64, clear, 0)
-    bit = 8 * (iota((TR, 128), 0) // 6) + iota((TR, 128), 1) // 16
-    lane8, sub8 = iota((8, 128), 1), iota((8, 128), 0)
+def row_weights(rtap_ref, rowtaps):
+    for k in range(6):
+        taps = rtap_ref[k].astype(F32).T
+        rowtaps[k] = jnp.concatenate(
+            [taps[0:16], taps[16:32], taps[32:48], jnp.zeros((16, 56), F32)], axis=1
+        )
+
+
+def row_warp(p0, p1, shifts_s, rowtaps, half):
     lane1 = iota((1, 128), 1)
     third_of, row_of = lane1 // TR, lane1 % TR
     rr = iota((72, 128), 0)
@@ -164,45 +161,65 @@
         ).astype(BF16)
         shift = jnp.where(
             third_of == 0,
-            shifts_s[n, 0],
-            jnp.where(third_of == 1, shifts_s[n + 16, 0], shifts_s[n + 32, 0]),
+            shifts_s[0, n],
+            jnp.where(third_of == 1, shifts_s[0, n + 16], shifts_s[0, n + 32]),
         )
         base = third_of * TR + jnp.clip(row_of + shift - 3, 0, TR - 6)
         delta = rr - jnp.broadcast_to(base, (72, 128))
-        taps = rowtaps[pl.ds(pl.multiple_of(8 * n, 8), 8), :]
         band = jnp.zeros((72, 128), F32)
         for k in range(6):
-            band = jnp.where(delta == k, jnp.broadcast_to(taps[k : k + 1], (72, 128)), band)
-        half = lax.dot_general(
+            taps = jnp.broadcast_to(rowtaps[k, pl.ds(n, 1), :], (72, 128))
+            band = jnp.where(delta == k, taps, band)
+        out = lax.dot_general(
             band.astype(BF16), stack, (((0,), (0,)), ((), ())), preferred_element_type=F32
         )
+        half[n] = out[:72]
+        return carry
+
+    lax.fori_loop(0, TRIOS, trio, 0, unroll=UNROLL_A)
+
+
+def place_tiles(half, words_s, weights_s, dest_s, slot_s, diag, count, heads, planes_ref):
+    bit = 8 * (iota((TR, 128), 0) // 6) + iota((TR, 128), 1) // 16
+    lane1 = iota((1, 128), 1)
+
+    def trio(n, carry):
         for third in range(3):
             t = n + 16 * third
-            h = half[TR * third : TR * third + TR]
-            acc = jnp.zeros((TR, 128), F32)
-            for o in range(-SPAN, SPAN + 1):
-                d = diag[o + SPAN, pl.ds(t, 1), :]
-                moved = pltpu.roll(h, (-o) % 128, 1) if o else h
-                acc = acc + jnp.broadcast_to(d, (TR, 128)) * moved
+            h = half[n, pl.ds(TR * third, TR), :]
+            acc = jnp.broadcast_to(diag[SPAN, pl.ds(t, 1), :], (TR, 128)) * h
+            for o in range(1, SPAN + 1):
+                for sign in (-o, o):
+                    d = jnp.broadcast_to(diag[sign + SPAN, pl.ds(t, 1), :], (TR, 128))
+                    acc = acc + d * pltpu.roll(h, (-sign) % 128, 1)
             word, weight = words_s[t], weights_s[t]
             flagged = lax.shift_right_logical(jnp.full((TR, 128), word, jnp.int32), bit) & 1
             prod = (acc * jnp.where(flagged == 0, weight, 0.0)).astype(BF16)
-            to = dest_s[t, 0]
+            to = dest_s[0, t]
             rank = count[to]
             count[to] = rank + 1
-            for a in range(3):
-                out_ref[to, 3 * rank + a] = prod[8 * a : 8 * a + 8]
-            flag8 = lax.shift_right_logical(jnp.full((8, 128), word, jnp.int32), lane8 & 31) & 1
-            head = jnp.where(
-                lane8 < 32,
-                jnp.where(flag8 == 0, weight, 0.0),
-                jnp.where(lane8 == 32, jnp.full((8, 128), slot_s[t], jnp.int32).astype(F32), 0.0),
+            at = 2 * to + rank
+            planes_ref[at] = prod
+            flag1 = lax.shift_right_logical(jnp.full((1, 128), word, jnp.int32), lane1 & 31) & 1
+            heads[pl.ds(at, 1), :] = jnp.where(
+                lane1 < 32,
+                jnp.where(flag1 == 0, weight, 0.0),
+                jnp.where(lane1 == 32, jnp.full((1, 128), slot_s[t], jnp.int32).astype(F32), 0.0),
             )
-            old = out_ref[to, 6].astype(F32)
-            out_ref[to, 6] = jnp.where(sub8 == rank, head, old).astype(BF16)
         return carry
 
-    lax.fori_loop(0, TRIOS, trio, 0)
+    lax.fori_loop(0, TRIOS, trio, 0, unroll=UNROLL_B)
+
+
+def clear_blocks(count, heads, planes_ref):
+    planes_ref[...] = jnp.zeros(planes_ref.shape, BF16)
+    heads[...] = jnp.zeros(heads.shape, F32)
+
+    def clear(d, carry):
+        count[d] = 0
+        return carry
+
+    lax.fori_loop(0, 64, clear, 0, unroll=8)
 
 
 def send_kernel(
@@ -212,13 +229,16 @@
     slot_s,
     shifts_s,
     coef_s,
-    shiftv_ref,
-    tiles_ref,
+    shifts_ref,
     rtap_ref,
     ctap_ref,
     brow_ref,
     bcol_ref,
-    out_ref,
+    tiles_hbm,
+    planes_ref,
+    heads_ref,
+    tiles,
+    sems,
     flat,
     image,
     pad,
@@ -229,21 +249,34 @@
     s1,
     p0,
     p1,
-    taps,
     rowtaps,
     diag,
+    half,
+    heads,
     count,
 ):
-    unpack_tiles(tiles_ref, flat, image)
+    copies = []
+    for octet in range(6):
+        rows = pl.ds(8 * octet, 8)
+        copies.append(
+            pltpu.make_async_copy(tiles_hbm.at[rows, :], tiles.at[rows, :], sems.at[octet])
+        )
+        copies[-1].start()
     make_tables(brow_ref, bcol_ref, pad, rtab, w0, w1)
-    column_weights(ctap_ref, shiftv_ref, taps, diag)
+    column_weights(ctap_ref, shifts_ref, diag)
     row_weights(rtap_ref, rowtaps)
+    clear_blocks(count, heads, planes_ref)
+    unpack_tiles(tiles, copies, flat, image)
     row_stage(image, rtab, coef_s, s0, s1)
     p0[...] = jnp.dot(s0[...], w0[...], preferred_element_type=F32)
     p1[...] = jnp.dot(s1[...], w1[...], preferred_element_type=F32)
-    warp_stage(
-        p0, p1, shifts_s, words_s, weights_s, dest_s, slot_s, rowtaps, diag, count, out_ref
-    )
+    row_warp(p0, p1, shifts_s, rowtaps, half)
+    place_tiles(half, words_s, weights_s, dest_s, slot_s, diag, count, heads, planes_ref)
+    heads_ref[...] = heads[...].astype(BF16)
+
+
+UNROLL_A = 4
+UNROLL_B = 2
 
 
 def send_blocks(tiles, coef, rtap, ctap, shifts, words, weights, dest, slot, brow, bcol):
@@ -251,10 +284,15 @@
     vmem = pl.BlockSpec(memory_space=pltpu.VMEM)
     return pl.pallas_call(
         send_kernel,
-        out_shape=jax.ShapeDtypeStruct((64, 7, 8, 128), BF16),
-        in_specs=[smem] * 6 + [vmem] * 6,
-        out_specs=vmem,
+        out_shape=(
+            jax.ShapeDtypeStruct((128, TR, TC), BF16),
+            jax.ShapeDtypeStruct((128, 128), BF16),
+        ),
+        in_specs=[smem] * 6 + [vmem] * 5 + [pl.BlockSpec(memory_space=pltpu.HBM)],
+        out_specs=(vmem, vmem),
         scratch_shapes=[
+            pltpu.VMEM((48, IR * IC), BF16),
+            pltpu.SemaphoreType.DMA((6,)),
             pltpu.VMEM((48 * 84 + 8, 128), F32),
             pltpu.VMEM((4 * TRIOS * IR, 128), F32),
             pltpu.VMEM((32, 128), F32),
@@ -265,14 +303,28 @@
             pltpu.VMEM((384, NB * 256), BF16),
             pltpu.VMEM((384, 256), F32),
             pltpu.VMEM((384, 256), F32),
-            pltpu.VMEM((48 * 8, 128), F32),
-            pltpu.VMEM((TRIOS * 8, 128), F32),
+            pltpu.VMEM((6, TRIOS, 128), F32),
             pltpu.VMEM((2 * SPAN + 1, 48, 128), F32),
+            pltpu.VMEM((TRIOS, 72, 128), F32),
+            pltpu.VMEM((128, 128), F32),
             pltpu.SMEM((64,), jnp.int32),
         ],
-        compiler_params=pltpu.CompilerParams(vmem_limit_bytes=50 << 20),
+        compiler_params=pltpu.CompilerParams(vmem_limit_bytes=67043328),
         name="match_and_warp",
-    )(words, weights.astype(F32), dest, slot, shifts, coef, shifts, tiles, rtap, ctap, brow, bcol)
+    )(
+        words,
+        weights.astype(F32),
+        dest.T,
+        slot,
+        shifts.T,
+        coef.T,
+        shifts.T,
+        rtap.transpose(1, 2, 0),
+        ctap.transpose(1, 0, 2),
+        brow,
+        bcol,
+        tiles,
+    )
 
 
 def body(
@@ -288,7 +340,7 @@
     basis_rows,
     basis_cols,
 ):
-    send = send_blocks(
+    planes, heads = send_blocks(
         padded_tiles,
         coefficients,
         row_taps,
@@ -300,21 +352,19 @@
         patch_slot,
         basis_rows,
         basis_cols,
-    ).reshape(64, 56, 128)
+    )
+    send = jnp.concatenate([planes.reshape(64, 2, TR * TC), heads.reshape(64, 2, 128)], axis=2)
     recv = lax.all_to_all(send, "sky", split_axis=0, concat_axis=0, tiled=True)
-    planes = recv[:, :48].reshape(128, TR * TC)
-    heads = recv[:, 48:50].reshape(128, 128)
-    slot_of = heads[:, 32].astype(jnp.int32)
+    recv = recv.reshape(128, TR * TC + 128)
+    slot_of = recv[:, TR * TC + 32].astype(jnp.int32)
     pick = (iota((16, 128), 0) == slot_of[None, :]).astype(BF16)
-    sums = jnp.dot(pick, planes, preferred_element_type=F32).astype(BF16)
-    cells = jnp.dot(pick, heads, preferred_element_type=F32).astype(BF16)
-    parts = jnp.concatenate(
-        [sums.reshape(8, 48, 128), cells.reshape(8, 2, 128), jnp.zeros((8, 6, 128), BF16)], axis=1
-    )
+    sums = jnp.dot(pick, recv, preferred_element_type=F32).astype(BF16)
+    parts = sums.reshape(8, 2, TR * TC + 128)
     parts = lax.all_to_all(parts, "exp", split_axis=0, concat_axis=0, tiled=True)
     totals = jnp.sum(parts.astype(F32), axis=0)
-    weight_sum = spread_cells(totals[48:50, :32]).reshape(48, 128)
-    return totals[:48] / jnp.maximum(weight_sum, 1.0)
+    numerator = totals[:, : TR * TC].reshape(2 * TR, TC)
+    weight_sum = spread_cells(totals[:, TR * TC : TR * TC + 32]).reshape(2 * TR, TC)
+    return numerator / jnp.maximum(weight_sum, 1.0)
 
 
 def spread_cells(cells):

time: 80.3 us -> 73.3 us (0.913)
  blocking collectives: 15.5 us -> 53.2 us
  waiting for transfers between devices: 25.5 us -> 0 us
  starting transfers between devices: 14.3 us -> 0 us
  local copies, waits for them, and re-layouts: 6.61 us -> 3.02 us
  Pallas kernels: 16.6 us -> 13.7 us
  other arithmetic: 0.94 us -> 2.82 us
    all_to_all x0 -> x1, blocking collectives: none -> 37.6 us  [body(): recv = lax.all_to_all(send, 'sky', split_axis=0, concat_axis=0, tiled=True)]
    all_to_all x1 -> x0, waiting for transfers between devices: 25.5 us -> none  [body(): recv = lax.all_to_all(send, 'sky', split_axis=0, concat_axis=0, tiled=True)]
    all_to_all x1 -> x0, starting transfers between devices: 14.3 us -> none  [body(): recv = lax.all_to_all(send, 'sky', split_axis=0, concat_axis=0, tiled=True)]
    unnamed x25 -> x2, local copies, waits for them, and re-layouts: 5.48 us -> 0.01 us
    pallas_call x1, Pallas kernels: 16.6 us -> 13.7 us  [send_blocks(): pl.pallas_call(send_kernel, out_shape=(jax.ShapeDtypeStruct((128, TR, TC)...]
    reshape x2 -> x4, local copies, waits for them, and re-layouts: 0.39 us -> 2.44 us  [the longest x1 2.05 us: body(): planes.reshape(64, 2, TR * TC)]
    convert_element_type x1, other arithmetic: 0.01 us -> 1.17 us  [send_blocks(): weights.astype(F32)]
  transfers between devices with their start and end apart: 1 -> 0, of which waited for: 1 -> 0; matrix products, arithmetic and copies ran while one was open for 0% -> 0% of each run, Pallas kernels for 0% -> 0%
where the time goes in v3:
time: 73.3 us; the launch traced here: 73 us
  blocking collectives  53.2 us (73%)
  Pallas kernels  13.7 us (19%)
  local copies, waits for them, and re-layouts  3.02 us (4%)
  other arithmetic  2.82 us (4%)
    all_to_all x1, blocking collectives, body(): recv = lax.all_to_all(send, 'sky', split_axis=0, concat_axis=0, tiled=True)  37.6 us
    all_to_all x1, blocking collectives, body(): lax.all_to_all(parts, 'exp', split_axis=0, concat_axis=0, tiled=True)  15.6 us
    pallas_call x1, Pallas kernels, send_blocks(): pl.pallas_call(send_kernel, out_shape=(jax.ShapeDtypeStruct((128, TR, TC)...  13.7 us
    reshape x1, local copies, waits for them, and re-layouts, body(): planes.reshape(64, 2, TR * TC)  2.05 us

profile of v3, /device:TPU:7, one launch (start us, length us, event | category | flops | bytes accessed | tf_op | source)
XLA Modules:
  0.0 73.0 jit_solution(18183052220399727582)
XLA Ops:
  0.0 1.2 %convert_element_type.20.weights_s = f32[48]{0:T(128)} convert(bf16[48]{0:T(256)(128)(2,1)} %param.17) | non-fusion elementwise | flops 48 | bytes 288 | tf_op jit(solution)/shard_map/convert_element_type | solution.py:316
  1.2 13.7 %match_and_warp.1 = (bf16[128,24,128]{2,1,0:T(8,128)(2,1)}, bf16[128,128]{1,0:T(8,128)(2,1)}) custom-call(s32[48]{0:T(128)} %words_s.1, f32[48]{0:T(128)} %convert_element_type.20.weights_s, s32[1,48]{1,0:T(1,128)} %bitcast.17, s32[48]{0:T(128)} %slot_s.1, s32[2,48]{1,0:T(2,128)} %bitcast.15, f32[20,48]{1,0:T(8,128)} %bitcast.14, s32[2,48]{1,0:T(2,128)} %bitcast.16, ...), custom_call_target="tpu_custom_call" | custom-call | tf_op jit(solution)/shard_map/match_and_warp/pallas_call | solution.py:285
  14.9 0.0 copy-start
  14.9 2.1 %reshape.30 = bf16[64,2,3072]{2,1,0:T(2,128)(2,1)S(1)} reshape(bf16[128,24,128]{2,1,0:T(8,128)(2,1)} %get-tuple-element.7) | data formatting | bytes 1572864 | tf_op jit(solution)/shard_map/reshape | solution.py:356
  16.9 0.0 copy-done
  17.0 0.7 %pad_maximum_fusion = bf16[64,2,3200]{2,1,0:T(2,128)(2,1)S(1)} fusion(bf16[64,2,128]{2,1,0:T(2,128)(2,1)S(1)} %bitcast.13, bf16[64,2,3072]{2,1,0:T(2,128)(2,1)S(1)} %reshape.30), kind=kLoop, calls=%fused_computation.1 | loop fusion | flops 1638400 | bytes 1638400 | tf_op jit(solution)/shard_map/concatenate | solution.py:356
  17.7 37.6 %all_to_all.10 = bf16[64,2,3200]{2,1,0:T(2,128)(2,1)S(1)} all-to-all(bf16[64,2,3200]{2,1,0:T(2,128)(2,1)S(1)} %pad_maximum_fusion), channel_id=1, replica_groups=mesh['sky'=64,'exp'=8] {'sky'}, dimensions={0} | all-to-all | bytes 1638400 | tf_op jit(solution)/shard_map/all_to_all | solution.py:357
  55.3 0.3 reshape.32
  55.6 0.2 convert_reduce_fusion.1
  55.8 0.2 convolution_convert_fusion
  56.0 0.1 reshape.33
  56.1 15.6 %all_to_all.11 = bf16[8,2,3200]{2,1,0:T(2,128)(2,1)S(1)} all-to-all(bf16[8,2,3200]{2,1,0:T(2,128)(2,1)S(1)} %reshape.33), channel_id=1, replica_groups=mesh['sky'=64,'exp'=8] {'exp'}, dimensions={0} | all-to-all | bytes 204800 | tf_op jit(solution)/shard_map/all_to_all | solution.py:363
  71.7 0.1 convert_reduce_fusion
  71.8 0.1 max.19
  71.9 0.1 copy.16
  72.0 0.1 broadcast_in_dim.7
  72.0 0.1 max.20
  72.2 0.1 max.21
  72.3 0.1 copy.18
  72.4 0.6 div.3
  (5 shorter events, 0.1 us)
Async XLA Ops:
  14.9 2.1 %copy-start = (bf16[128,128]{1,0:T(8,128)(2,1)S(1)}, bf16[128,128]{1,0:T(8,128)(2,1)}, u32[]{:S(2)}) copy-start(bf16[128,128]{1,0:T(8,128)(2,1)} %get-tuple-element.8) | copy-start | bytes 98308

commit v4 on v3

--- a/solution.py
+++ b/solution.py
@@ -15,6 +15,7 @@
 IR = TR + KW - 1
 IC = TC + KW - 1
 SPAN = 5
+PITCH = 136
 
 
 def iota(shape, axis):
@@ -123,14 +124,17 @@
     lax.fori_loop(0, TRIOS // 2, step, 0)
 
 
-def column_weights(ctap_ref, shifts_ref, diag):
+def lane_copies(row):
+    own = jnp.where(
+        iota((48, 48), 0) == iota((48, 48), 1), jnp.broadcast_to(row, (48, 48)), 0.0
+    )
+    return jnp.dot(own.astype(BF16), jnp.ones((48, 128), BF16), preferred_element_type=F32)
+
+
+def column_weights(ctap_ref, shifts_ref, weights_ref, diag, tile_weights):
+    tile_weights[...] = lane_copies(weights_ref[...].astype(F32))
     j = iota((48, 128), 1)
-    own = jnp.where(
-        iota((48, 48), 0) == iota((48, 48), 1),
-        jnp.broadcast_to(shifts_ref[1:2, :], (48, 48)).astype(F32),
-        0.0,
-    )
-    shift = jnp.dot(own.astype(BF16), jnp.ones((48, 128), BF16), preferred_element_type=F32)
+    shift = lane_copies(shifts_ref[1:2, :].astype(F32))
     offset = jnp.clip(j + shift.astype(jnp.int32) - 3, 0, TC - 6) - j
     kept = [ctap_ref[k].astype(F32) for k in range(6)]
     for o in range(-SPAN, SPAN + 1):
@@ -179,7 +183,7 @@
     lax.fori_loop(0, TRIOS, trio, 0, unroll=UNROLL_A)
 
 
-def place_tiles(half, words_s, weights_s, dest_s, slot_s, diag, count, heads, planes_ref):
+def place_tiles(half, words_s, dest_s, slot_s, diag, tile_weights, count, blocks):
     bit = 8 * (iota((TR, 128), 0) // 6) + iota((TR, 128), 1) // 16
     lane1 = iota((1, 128), 1)
 
@@ -192,16 +196,16 @@
                 for sign in (-o, o):
                     d = jnp.broadcast_to(diag[sign + SPAN, pl.ds(t, 1), :], (TR, 128))
                     acc = acc + d * pltpu.roll(h, (-sign) % 128, 1)
-            word, weight = words_s[t], weights_s[t]
+            word, weight = words_s[t], tile_weights[pl.ds(t, 1), :]
             flagged = lax.shift_right_logical(jnp.full((TR, 128), word, jnp.int32), bit) & 1
-            prod = (acc * jnp.where(flagged == 0, weight, 0.0)).astype(BF16)
+            prod = acc * jnp.where(flagged == 0, jnp.broadcast_to(weight, (TR, 128)), 0.0)
             to = dest_s[0, t]
             rank = count[to]
             count[to] = rank + 1
             at = 2 * to + rank
-            planes_ref[at] = prod
+            blocks[pl.ds(at, TR, stride=PITCH), :] = prod
             flag1 = lax.shift_right_logical(jnp.full((1, 128), word, jnp.int32), lane1 & 31) & 1
-            heads[pl.ds(at, 1), :] = jnp.where(
+            blocks[pl.ds(TR * PITCH + at, 1), :] = jnp.where(
                 lane1 < 32,
                 jnp.where(flag1 == 0, weight, 0.0),
                 jnp.where(lane1 == 32, jnp.full((1, 128), slot_s[t], jnp.int32).astype(F32), 0.0),
@@ -211,9 +215,8 @@
     lax.fori_loop(0, TRIOS, trio, 0, unroll=UNROLL_B)
 
 
-def clear_blocks(count, heads, planes_ref):
-    planes_ref[...] = jnp.zeros(planes_ref.shape, BF16)
-    heads[...] = jnp.zeros(heads.shape, F32)
+def clear_blocks(count, blocks):
+    blocks[...] = jnp.zeros(blocks.shape, F32)
 
     def clear(d, carry):
         count[d] = 0
@@ -224,19 +227,18 @@
 
 def send_kernel(
     words_s,
-    weights_s,
     dest_s,
     slot_s,
     shifts_s,
     coef_s,
     shifts_ref,
+    weights_ref,
     rtap_ref,
     ctap_ref,
     brow_ref,
     bcol_ref,
     tiles_hbm,
-    planes_ref,
-    heads_ref,
+    out_ref,
     tiles,
     sems,
     flat,
@@ -252,7 +254,8 @@
     rowtaps,
     diag,
     half,
-    heads,
+    tile_weights,
+    blocks,
     count,
 ):
     copies = []
@@ -263,16 +266,17 @@
         )
         copies[-1].start()
     make_tables(brow_ref, bcol_ref, pad, rtab, w0, w1)
-    column_weights(ctap_ref, shifts_ref, diag)
+    column_weights(ctap_ref, shifts_ref, weights_ref, diag, tile_weights)
     row_weights(rtap_ref, rowtaps)
-    clear_blocks(count, heads, planes_ref)
+    clear_blocks(count, blocks)
     unpack_tiles(tiles, copies, flat, image)
     row_stage(image, rtab, coef_s, s0, s1)
     p0[...] = jnp.dot(s0[...], w0[...], preferred_element_type=F32)
     p1[...] = jnp.dot(s1[...], w1[...], preferred_element_type=F32)
     row_warp(p0, p1, shifts_s, rowtaps, half)
-    place_tiles(half, words_s, weights_s, dest_s, slot_s, diag, count, heads, planes_ref)
-    heads_ref[...] = heads[...].astype(BF16)
+    place_tiles(half, words_s, dest_s, slot_s, diag, tile_weights, count, blocks)
+    for i in range(TR + 1):
+        out_ref[:, pl.ds(128 * i, 128)] = blocks[pl.ds(PITCH * i, 128), :].astype(BF16)
 
 
 UNROLL_A = 4
@@ -284,12 +288,9 @@
     vmem = pl.BlockSpec(memory_space=pltpu.VMEM)
     return pl.pallas_call(
         send_kernel,
-        out_shape=(
-            jax.ShapeDtypeStruct((128, TR, TC), BF16),
-            jax.ShapeDtypeStruct((128, 128), BF16),
-        ),
-        in_specs=[smem] * 6 + [vmem] * 5 + [pl.BlockSpec(memory_space=pltpu.HBM)],
-        out_specs=(vmem, vmem),
+        out_shape=jax.ShapeDtypeStruct((128, (TR + 1) * 128), BF16),
+        in_specs=[smem] * 5 + [vmem] * 6 + [pl.BlockSpec(memory_space=pltpu.HBM)],
+        out_specs=vmem,
         scratch_shapes=[
             pltpu.VMEM((48, IR * IC), BF16),
             pltpu.SemaphoreType.DMA((6,)),
@@ -306,19 +307,20 @@
             pltpu.VMEM((6, TRIOS, 128), F32),
             pltpu.VMEM((2 * SPAN + 1, 48, 128), F32),
             pltpu.VMEM((TRIOS, 72, 128), F32),
-            pltpu.VMEM((128, 128), F32),
+            pltpu.VMEM((48, 128), F32),
+            pltpu.VMEM(((TR + 1) * PITCH, 128), F32),
             pltpu.SMEM((64,), jnp.int32),
         ],
         compiler_params=pltpu.CompilerParams(vmem_limit_bytes=67043328),
         name="match_and_warp",
     )(
         words,
-        weights.astype(F32),
         dest.T,
         slot,
         shifts.T,
         coef.T,
         shifts.T,
+        weights.reshape(1, 48),
         rtap.transpose(1, 2, 0),
         ctap.transpose(1, 0, 2),
         brow,
@@ -340,7 +342,7 @@
     basis_rows,
     basis_cols,
 ):
-    planes, heads = send_blocks(
+    blocks = send_blocks(
         padded_tiles,
         coefficients,
         row_taps,
@@ -353,7 +355,7 @@
         basis_rows,
         basis_cols,
     )
-    send = jnp.concatenate([planes.reshape(64, 2, TR * TC), heads.reshape(64, 2, 128)], axis=2)
+    send = blocks.reshape(64, 2, TR * TC + 128)
     recv = lax.all_to_all(send, "sky", split_axis=0, concat_axis=0, tiled=True)
     recv = recv.reshape(128, TR * TC + 128)
     slot_of = recv[:, TR * TC + 32].astype(jnp.int32)

time: 73.3 us -> 71.4 us (0.974)
  other arithmetic: 2.82 us -> 0.91 us
    convert_element_type x1 -> x0, other arithmetic: 1.17 us -> none  [send_blocks(): weights.astype(F32)]
    concatenate x1 -> x0, other arithmetic: 0.74 us -> none  [body(): jnp.concatenate([planes.reshape(64, 2, TR * TC), heads.reshape(64, 2, 128...]
where the time goes in v4:
time: 71.4 us; the launch traced here: 71.2 us
  blocking collectives  53.2 us (75%)
  Pallas kernels  13.6 us (19%)
  local copies, waits for them, and re-layouts  3.18 us (4%)
  other arithmetic  0.91 us (1%)
    all_to_all x1, blocking collectives, body(): recv = lax.all_to_all(send, 'sky', split_axis=0, concat_axis=0, tiled=True)  37.6 us
    all_to_all x1, blocking collectives, body(): lax.all_to_all(parts, 'exp', split_axis=0, concat_axis=0, tiled=True)  15.6 us
    pallas_call x1, Pallas kernels, send_blocks(): pl.pallas_call(send_kernel, out_shape=jax.ShapeDtypeStruct((128, (TR + 1)...  13.6 us
    reshape x1, local copies, waits for them, and re-layouts, body(): send = blocks.reshape(64, 2, TR * TC + 128)  2.22 us

profile of v4, /device:TPU:7, one launch (start us, length us, event | category | flops | bytes accessed | tf_op | source)
XLA Modules:
  0.0 71.2 jit_solution(3282675521447831604)
XLA Ops:
  0.0 13.6 %match_and_warp.1 = bf16[128,3200]{1,0:T(8,128)(2,1)} custom-call(s32[48]{0:T(128)} %words_s.1, s32[1,48]{1,0:T(1,128)} %bitcast.16, s32[48]{0:T(128)} %slot_s.1, s32[2,48]{1,0:T(2,128)} %bitcast.14, f32[20,48]{1,0:T(8,128)} %bitcast.13, s32[2,48]{1,0:T(2,128)} %bitcast.15, bf16[1,48]{1,0:T(2,128)(2,1)} %bitcast.17, bf16[6,24,48]{2,1,0:T(8,128)(2,1)} %bitcast.12, ...), custom_call_target="tpu_custom_call" | custom-call | tf_op jit(solution)/shard_map/match_and_warp/pallas_call | solution.py:289
  13.6 2.2 %reshape.31 = bf16[64,2,3200]{2,1,0:T(2,128)(2,1)S(1)} reshape(bf16[128,3200]{1,0:T(8,128)(2,1)} %match_and_warp.1) | data formatting | bytes 1638400 | tf_op jit(solution)/shard_map/reshape | solution.py:358
  15.9 37.6 %all_to_all.10 = bf16[64,2,3200]{2,1,0:T(2,128)(2,1)S(1)} all-to-all(bf16[64,2,3200]{2,1,0:T(2,128)(2,1)S(1)} %reshape.31), channel_id=1, replica_groups=mesh['sky'=64,'exp'=8] {'sky'}, dimensions={0} | all-to-all | bytes 1638400 | tf_op jit(solution)/shard_map/all_to_all | solution.py:359
  53.5 0.3 reshape.32
  53.8 0.2 convert_reduce_fusion.1
  53.9 0.2 convolution_convert_fusion
  54.2 0.1 reshape.33
  54.2 15.6 %all_to_all.11 = bf16[8,2,3200]{2,1,0:T(2,128)(2,1)S(1)} all-to-all(bf16[8,2,3200]{2,1,0:T(2,128)(2,1)S(1)} %reshape.33), channel_id=1, replica_groups=mesh['sky'=64,'exp'=8] {'exp'}, dimensions={0} | all-to-all | bytes 204800 | tf_op jit(solution)/shard_map/all_to_all | solution.py:365
  69.8 0.1 convert_reduce_fusion
  70.0 0.1 max.19
  70.0 0.1 copy.16
  70.1 0.1 broadcast_in_dim.7
  70.2 0.1 max.20
  70.4 0.1 max.21
  70.5 0.1 copy.18
  70.5 0.6 div.3
  (5 shorter events, 0.1 us)

commit v5 on v4

--- a/solution.py
+++ b/solution.py
@@ -279,8 +279,8 @@
         out_ref[:, pl.ds(128 * i, 128)] = blocks[pl.ds(PITCH * i, 128), :].astype(BF16)
 
 
-UNROLL_A = 4
-UNROLL_B = 2
+UNROLL_A = 8
+UNROLL_B = 4
 
 
 def send_blocks(tiles, coef, rtap, ctap, shifts, words, weights, dest, slot, brow, bcol):
@@ -288,7 +288,7 @@
     vmem = pl.BlockSpec(memory_space=pltpu.VMEM)
     return pl.pallas_call(
         send_kernel,
-        out_shape=jax.ShapeDtypeStruct((128, (TR + 1) * 128), BF16),
+        out_shape=pltpu.VMEM((128, (TR + 1) * 128), BF16),
         in_specs=[smem] * 5 + [vmem] * 6 + [pl.BlockSpec(memory_space=pltpu.HBM)],
         out_specs=vmem,
         scratch_shapes=[
@@ -311,7 +311,7 @@
             pltpu.VMEM(((TR + 1) * PITCH, 128), F32),
             pltpu.SMEM((64,), jnp.int32),
         ],
-        compiler_params=pltpu.CompilerParams(vmem_limit_bytes=67043328),
+        compiler_params=pltpu.CompilerParams(vmem_limit_bytes=65994752),
         name="match_and_warp",
     )(
         words,

time: 71.4 us -> 68 us (0.952)
  local copies, waits for them, and re-layouts: 3.18 us -> 1.27 us
  Pallas kernels: 13.6 us -> 12.1 us
    reshape x1, local copies, waits for them, and re-layouts: 2.22 us -> 0.31 us  [body(): send = blocks.reshape(64, 2, TR * TC + 128)]
    pallas_call x1, Pallas kernels: 13.6 us -> 12.1 us  [send_blocks(): pl.pallas_call(send_kernel, out_shape=pltpu.VMEM((128, (TR + 1) * 128), B...]
where the time goes in v5:
time: 68 us; the launch traced here: 67.8 us
  blocking collectives  53.2 us (78%)
  Pallas kernels  12.1 us (18%)
  local copies, waits for them, and re-layouts  1.27 us (2%)
  other arithmetic  0.91 us (1%)
    all_to_all x1, blocking collectives, body(): recv = lax.all_to_all(send, 'sky', split_axis=0, concat_axis=0, tiled=True)  37.6 us
    all_to_all x1, blocking collectives, body(): lax.all_to_all(parts, 'exp', split_axis=0, concat_axis=0, tiled=True)  15.6 us
    pallas_call x1, Pallas kernels, send_blocks(): pl.pallas_call(send_kernel, out_shape=pltpu.VMEM((128, (TR + 1) * 128), B...  12.1 us

profile of v5, /device:TPU:7, one launch (start us, length us, event | category | flops | bytes accessed | tf_op | source)
XLA Modules:
  0.0 67.8 jit_solution(12345917135721762595)
XLA Ops:
  0.0 12.1 %match_and_warp.1 = bf16[128,3200]{1,0:T(8,128)(2,1)S(1)} custom-call(s32[48]{0:T(128)} %words_s.1, s32[1,48]{1,0:T(1,128)} %bitcast.16, s32[48]{0:T(128)} %slot_s.1, s32[2,48]{1,0:T(2,128)} %bitcast.14, f32[20,48]{1,0:T(8,128)} %bitcast.13, s32[2,48]{1,0:T(2,128)} %bitcast.15, bf16[1,48]{1,0:T(2,128)(2,1)} %bitcast.17, bf16[6,24,48]{2,1,0:T(8,128)(2,1)} %bitcast.12, ...), custom_call_target="tpu_custom_call" | custom-call | tf_op jit(solution)/shard_map/match_and_warp/pallas_call | solution.py:289
  12.1 0.3 reshape.31
  12.4 37.6 %all_to_all.10 = bf16[64,2,3200]{2,1,0:T(2,128)(2,1)S(1)} all-to-all(bf16[64,2,3200]{2,1,0:T(2,128)(2,1)S(1)} %reshape.31), channel_id=1, replica_groups=mesh['sky'=64,'exp'=8] {'sky'}, dimensions={0} | all-to-all | bytes 1638400 | tf_op jit(solution)/shard_map/all_to_all | solution.py:359
  50.0 0.3 reshape.32
  50.4 0.2 convert_reduce_fusion.1
  50.5 0.2 convolution_convert_fusion
  50.8 0.1 reshape.33
  50.8 15.6 %all_to_all.11 = bf16[8,2,3200]{2,1,0:T(2,128)(2,1)S(1)} all-to-all(bf16[8,2,3200]{2,1,0:T(2,128)(2,1)S(1)} %reshape.33), channel_id=1, replica_groups=mesh['sky'=64,'exp'=8] {'exp'}, dimensions={0} | all-to-all | bytes 204800 | tf_op jit(solution)/shard_map/all_to_all | solution.py:365
  66.4 0.1 convert_reduce_fusion
  66.5 0.1 max.19
  66.6 0.1 copy.16
  66.7 0.1 broadcast_in_dim.7
  66.8 0.1 max.20
  66.9 0.1 max.21
  67.1 0.1 copy.18
  67.1 0.6 div.3
  (5 shorter events, 0.1 us)

commit v6 on v5

--- a/solution.py
+++ b/solution.py
@@ -279,7 +279,7 @@
         out_ref[:, pl.ds(128 * i, 128)] = blocks[pl.ds(PITCH * i, 128), :].astype(BF16)
 
 
-UNROLL_A = 8
+UNROLL_A = 16
 UNROLL_B = 4
 
 
@@ -294,8 +294,8 @@
         scratch_shapes=[
             pltpu.VMEM((48, IR * IC), BF16),
             pltpu.SemaphoreType.DMA((6,)),
-            pltpu.VMEM((48 * 84 + 8, 128), F32),
-            pltpu.VMEM((4 * TRIOS * IR, 128), F32),
+            pltpu.VMEM((48 * 84 + 96, 128), F32),
+            pltpu.VMEM((4 * TRIOS * IR + 16, 128), F32),
             pltpu.VMEM((32, 128), F32),
             pltpu.VMEM((NB * TR, 128), F32),
             pltpu.VMEM((NB * 256, 256), BF16),
@@ -308,7 +308,7 @@
             pltpu.VMEM((2 * SPAN + 1, 48, 128), F32),
             pltpu.VMEM((TRIOS, 72, 128), F32),
             pltpu.VMEM((48, 128), F32),
-            pltpu.VMEM(((TR + 1) * PITCH, 128), F32),
+            pltpu.VMEM(((TR + 2) * PITCH, 128), F32),
             pltpu.SMEM((64,), jnp.int32),
         ],
         compiler_params=pltpu.CompilerParams(vmem_limit_bytes=65994752),

time: 68 us -> 67.6 us (level)
  no operation moved by 1% of the time
where the time goes in v6:
time: 67.6 us; the launch traced here: 67.4 us
  blocking collectives  53.2 us (79%)
  Pallas kernels  11.8 us (17%)
  local copies, waits for them, and re-layouts  1.27 us (2%)
  other arithmetic  0.91 us (1%)
    all_to_all x1, blocking collectives, body(): recv = lax.all_to_all(send, 'sky', split_axis=0, concat_axis=0, tiled=True)  37.6 us
    all_to_all x1, blocking collectives, body(): lax.all_to_all(parts, 'exp', split_axis=0, concat_axis=0, tiled=True)  15.6 us
    pallas_call x1, Pallas kernels, send_blocks(): pl.pallas_call(send_kernel, out_shape=pltpu.VMEM((128, (TR + 1) * 128), B...  11.8 us

profile of v6, /device:TPU:7, one launch (start us, length us, event | category | flops | bytes accessed | tf_op | source)
XLA Modules:
  0.0 67.4 jit_solution(1929757813642089271)
XLA Ops:
  0.0 11.8 %match_and_warp.1 = bf16[128,3200]{1,0:T(8,128)(2,1)S(1)} custom-call(s32[48]{0:T(128)} %words_s.1, s32[1,48]{1,0:T(1,128)} %bitcast.16, s32[48]{0:T(128)} %slot_s.1, s32[2,48]{1,0:T(2,128)} %bitcast.14, f32[20,48]{1,0:T(8,128)} %bitcast.13, s32[2,48]{1,0:T(2,128)} %bitcast.15, bf16[1,48]{1,0:T(2,128)(2,1)} %bitcast.17, bf16[6,24,48]{2,1,0:T(8,128)(2,1)} %bitcast.12, ...), custom_call_target="tpu_custom_call" | custom-call | tf_op jit(solution)/shard_map/match_and_warp/pallas_call | solution.py:289
  11.8 0.3 reshape.31
  12.1 37.6 %all_to_all.10 = bf16[64,2,3200]{2,1,0:T(2,128)(2,1)S(1)} all-to-all(bf16[64,2,3200]{2,1,0:T(2,128)(2,1)S(1)} %reshape.31), channel_id=1, replica_groups=mesh['sky'=64,'exp'=8] {'sky'}, dimensions={0} | all-to-all | bytes 1638400 | tf_op jit(solution)/shard_map/all_to_all | solution.py:359
  49.7 0.3 reshape.32
  50.0 0.2 convert_reduce_fusion.1
  50.2 0.2 convolution_convert_fusion
  50.4 0.1 reshape.33
  50.5 15.6 %all_to_all.11 = bf16[8,2,3200]{2,1,0:T(2,128)(2,1)S(1)} all-to-all(bf16[8,2,3200]{2,1,0:T(2,128)(2,1)S(1)} %reshape.33), channel_id=1, replica_groups=mesh['sky'=64,'exp'=8] {'exp'}, dimensions={0} | all-to-all | bytes 204800 | tf_op jit(solution)/shard_map/all_to_all | solution.py:365
  66.0 0.1 convert_reduce_fusion
  66.2 0.1 max.19
  66.3 0.1 copy.16
  66.3 0.1 broadcast_in_dim.7
  66.4 0.1 max.20
  66.6 0.1 max.21
  66.7 0.1 copy.18
  66.8 0.6 div.3
  (5 shorter events, 0.1 us)
